TPU v7x, 32 devices: a whole 2x2x4 slice. The times are simulated.
32 devices in a mesh: ctx: 4 (over z), head: 8 (over y, x, core).
Axes of the slice: x: 2, y: 2, z: 4, core: 2. Of those that a mesh axis runs over, the one named last changes fastest.
Arguments:
- hidden: float32 [1024, 2304], P(('ctx', 'head')), may hold values from -40 to 40
- w_query: float32 [2304, 1536], P(None, 'head'), may hold values from -0.125 to 0.125
- w_down: float32 [2304, 576], replicated, may hold values from -0.125 to 0.125
- latent_gain: float32 [512], replicated, may hold values from 0.25 to 1.75
- w_key_up: float32 [512, 1024], P(None, 'head'), may hold values from -0.25 to 0.25
- w_value_up: float32 [512, 1024], P(None, 'head'), may hold values from -0.25 to 0.25
- w_out: float32 [1024, 2304], P('head'), may hold values from -0.1875 to 0.1875
Outputs:
- output: float32 [1024, 2304], P(('ctx', 'head'))
All inputs are finite; a program needn't handle non-finite values.
Results may differ from a plain program's by a relative error of at most 0.0003.
Values sent between devices are 32-bit elements; how exact they have to be, the bound alone decides.
A program may use at most 64 MiB of HBM per device.

v0:
```python
import functools

import jax
import jax.numpy as jnp
from jax import lax
from jax.experimental import pallas as pl
from jax.experimental.pallas import tpu as pltpu
from jax.sharding import PartitionSpec as P

EPSILON = 1e-06
FLOOR = -1e30
CORES = 2
MESH = pl.DeviceIdType.MESH
NN = (((1,), (0,)), ((), ()))
NT = (((1,), (1,)), ((), ()))


def halves(value):
    high = value.astype(jnp.bfloat16)
    return high, (value - high.astype(jnp.float32)).astype(jnp.bfloat16)


def product(left, right, dims=NN):
    (lh, ll), (rh, rl) = left, right
    dot = functools.partial(lax.dot_general, dimension_numbers=dims, preferred_element_type=jnp.float32)
    return dot(lh, rh) + (dot(ll, rh) + dot(lh, rl))


def kernel(
    ctx_n, chips, square, steps, pieces,
    hidden, w_query, w_down, gain, w_key, w_value, w_out, out,
    hid, wd, wq, gn, wk, wv, wo, lat, qh, ql, top, total, acc, part, landed,
    load_sem, swap_send, swap_recv, hid_send, hid_recv, col_send, col_recv,
    row_send, row_recv, twin_send, twin_recv, sum_send, sum_recv,
):
    rows, width = hidden.shape
    parts = 2 if square else 1
    rank = gn.shape[1]
    tail = wd.shape[0] - rank
    nope = wk.shape[2]
    per_core = chips * rows
    block = CORES * per_core
    lanes = lat.shape[1]
    ctx = lax.axis_index("ctx")
    head = lax.axis_index("head")
    chip, core = head // CORES, head % CORES
    twin = chip * CORES + (1 - core)

    def chip_at(offset):
        return lax.rem(chip + offset, chips)

    def to(o):
        if not square:
            return chip_at(o)
        return [chip, chip + 1 - 2 * lax.rem(chip, 2), lax.rem(chip + 2, 4), 3 - chip][o]

    def origin(o):
        return to(o) if square else chip_at(chips - o)

    def local(src, dst, sem):
        return pltpu.make_async_copy(src, dst, load_sem.at[sem])

    def remote(src, dst, send, recv, c, h):
        return pltpu.make_async_remote_copy(
            src_ref=src, dst_ref=dst, send_sem=send, recv_sem=recv,
            device_id={"ctx": c, "head": h}, device_id_type=MESH,
        )

    def at_rows(start, size):
        return pl.ds(pl.multiple_of(start, 8), size)

    my_hid = hid.at[at_rows(chip * rows, rows)]
    depth = width // steps
    loads = [local(hidden, my_hid, 0), local(gain, gn, 1)]
    for s in range(steps):
        span = pl.ds(s * depth, depth)
        loads.append(local(w_down.at[:, span], wd.at[:, span], 2 + s))
    pairs = [(w_query, wq), (w_key, wk), (w_value, wv), (w_out, wo)]
    own = [local(src, dst.at[core], 2 + steps + i) for i, (src, dst) in enumerate(pairs)]
    for copy in loads:
        copy.start()

    barrier = pltpu.get_barrier_semaphore()
    for o in range(1, chips):
        pl.semaphore_signal(barrier, inc=1, device_id={"ctx": ctx, "head": chip_at(o) * CORES + core}, device_id_type=MESH)
    pl.semaphore_signal(barrier, inc=1, device_id={"ctx": ctx, "head": twin}, device_id_type=MESH)
    for o in range(1, ctx_n):
        pl.semaphore_signal(barrier, inc=1, device_id={"ctx": lax.rem(ctx + o, ctx_n), "head": head}, device_id_type=MESH)
    pl.semaphore_wait(barrier, chips - 1 + 1 + ctx_n - 1)

    def share(source, spot, send, recv):
        def start_of(o, h):
            target = to(o)
            return remote(source(h), spot(chip, h), send(o, h), recv(o, h), ctx, target * CORES + core)

        def seen(o, h):
            place_of = spot(origin(o), h)
            return remote(place_of, place_of, send(o, h), recv(o, h), ctx, twin)

        def passed(h):
            place_of = spot(to(1 + h), h)
            return remote(place_of, place_of, send(3, h), recv(3, h), ctx, to(2 - h) * CORES + core)

        direct = [(1, 0), (2, 1), (1, 1), (2, 0)] if square else [(o, 0) for o in range(1, chips)]

        def start():
            for o, h in direct:
                start_of(o, h).start()

        def relay():
            if square:
                for h in range(2):
                    seen(1 + h, h).wait_recv()
                    passed(h).start()

        def finish():
            for o, h in [(1, 1), (2, 0), (3, 0), (3, 1)] if square else direct:
                seen(o, h).wait_recv()

        def drain():
            for o, h in direct:
                start_of(o, h).wait_send()
            if square:
                for h in range(2):
                    passed(h).wait_send()

        return start, relay, finish, drain

    half = width // parts

    def hid_half(h):
        return pl.ds(h * half, half)

    hid_start, hid_relay, hid_finish, hid_drain = share(
        lambda h: hidden.at[:, hid_half(h)],
        lambda k, h: hid.at[at_rows(k * rows, rows), hid_half(h)],
        lambda o, h: hid_send.at[o, h],
        lambda o, h: hid_recv.at[o, h],
    )
    hid_start()
    swaps = [remote(src, dst.at[core], swap_send.at[i], swap_recv.at[i], ctx, twin) for i, (src, dst) in enumerate(pairs)]
    for copy in own:
        copy.start()
    for copy in swaps:
        copy.start()

    loads[0].wait()
    loads[1].wait()
    down = jnp.zeros((rows, rank + tail), jnp.float32)
    for s in range(steps):
        loads[2 + s].wait()
        span = pl.ds(s * depth, depth)
        down += product(halves(my_hid[:, span]), halves(wd[:, span]), NT)
    raw = down[:, :rank]
    meansq = jnp.mean(raw * raw, axis=-1, keepdims=True)
    blank = jnp.zeros((rows, lanes - rank - tail), jnp.float32)

    def place(b, p, k):
        return ((b * CORES + p) * chips + k) * rows

    mine = at_rows(place(ctx, core, chip), rows)
    lat[mine, :rank] = raw * lax.rsqrt(meansq + EPSILON) * gn[...]
    lat[mine, rank:] = jnp.concatenate([down[:, rank:], blank], axis=1)

    def col_copy(b):
        spot = lat.at[at_rows(place(b, core, chip), rows)]
        return remote(spot, spot, col_send.at[b], col_recv.at[b], jnp.minimum(ctx + 1, ctx_n - 1), head)

    def latents(b):
        def spot(k, h):
            return lat.at[at_rows(place(b, core, k) + h * (rows // parts), rows // parts)]

        return share(
            lambda h: spot(chip, h), spot, lambda o, h: row_send.at[b, o, h], lambda o, h: row_recv.at[b, o, h]
        )

    def twin_copy(b, p):
        spot = lat.at[at_rows(place(b, p, 0), per_core)]
        return remote(spot, spot, twin_send.at[b], twin_recv.at[b], ctx, twin)

    def spread(b):
        @pl.when(ctx + 1 < ctx_n)
        def _():
            col_copy(b).start()

        latents(b)[0]()

    def gather_rows(b):
        latents(b)[2]()
        twin_copy(b, core).start()

    spread(ctx)
    hid_relay()
    for d in range(1, ctx_n):
        @pl.when(d <= ctx)
        def _():
            col_copy(ctx - d).wait_recv()
            spread(ctx - d)

    latents(ctx)[1]()

    hid_finish()
    for i in range(2):
        own[i].wait()
        swaps[i].wait()
    scale = wq.shape[1] ** (-0.5)
    pad = jnp.zeros((per_core, lanes - rank - tail), jnp.float32)
    query = [jnp.zeros((per_core, wq.shape[1]), jnp.float32) for _ in range(CORES)]
    for s in range(steps):
        span = pl.ds(s * depth, depth)
        piece = halves(hid[:, span])
        for p in range(CORES):
            query[p] += product(piece, halves(wq[p, :, span]), NT)
    for p in range(CORES):
        wide = product(halves(query[p][:, :nope] * scale), halves(wk[p]), NT)
        span = pl.ds(p * per_core, per_core)
        qh[span, :rank], ql[span, :rank] = halves(wide)
        qh[span, rank:], ql[span, rank:] = halves(jnp.concatenate([query[p][:, nope:] * scale, pad], axis=1))

    def spots(index, parity):
        inner = lax.rem(index, per_core)
        return (lax.div(inner, rows) * CORES + parity) * rows + lax.rem(inner, rows)

    def attend(b, first):
        keys = halves(lat[at_rows(place(b, 0, 0), block), :])
        scores = product((qh[...], ql[...]), keys, NT)
        if first:
            line = lax.broadcasted_iota(jnp.int32, (block, 1), 0)
            column = lax.broadcasted_iota(jnp.int32, (1, block), 1)
            causal = spots(line, core) >= spots(column, lax.div(column, per_core))
            scores = jnp.where(causal, scores, FLOOR)
            peak = jnp.max(scores, axis=1, keepdims=True)
        else:
            peak = jnp.maximum(top[...], jnp.max(scores, axis=1, keepdims=True))
        weights = jnp.exp(scores - peak)
        if first:
            weights = jnp.where(causal, weights, 0.0)
        mixed = product(halves(weights), (keys[0][:, :rank], keys[1][:, :rank]))
        added = jnp.sum(weights, axis=1, keepdims=True)
        if first:
            total[...] = added
            acc[...] = mixed
        else:
            fade = jnp.exp(top[...] - peak)
            total[...] = total[...] * fade + added
            acc[...] = acc[...] * fade + mixed
        top[...] = peak

    def relay_at(d):
        if d < ctx_n:
            @pl.when(d <= ctx)
            def _():
                latents(ctx - d)[1]()

    relay_at(1)
    gather_rows(ctx)
    twin_copy(ctx, 1 - core).wait_recv()
    attend(ctx, True)
    for d in range(1, ctx_n):
        @pl.when(d <= ctx)
        def _():
            relay_at(d + 1)
            gather_rows(ctx - d)
            twin_copy(ctx - d, 1 - core).wait_recv()
            attend(ctx - d, False)

    for i in range(2, 4):
        own[i].wait()
        swaps[i].wait()
    heads = []
    for p in range(CORES):
        span = pl.ds(p * per_core, per_core)
        heads.append(product(halves(acc[span, :] / total[span, :]), halves(wv[p])))
    attended = halves(jnp.concatenate(heads, axis=1))
    columns = width // pieces

    def cut(ref, k, t):
        return ref.at[at_rows(k * rows, rows), pl.ds(t * columns, columns)]

    def axes_of(t):
        return (1, 2) if t % 2 == 0 else (2, 1)

    def sum_copy(t, j):
        if not square:
            return remote(
                cut(part, chip_at(j), t), cut(landed, chip, t), sum_send.at[t, j], sum_recv.at[t, j],
                ctx, chip_at(j) * CORES + core,
            )
        first, second = axes_of(t)
        src = [to(3), to(first), to(second)][j]
        dst = [to(3), to(first), to(3)][j]
        target = [to(first), to(first), to(second)][j]
        return remote(cut(part, src, t), cut(landed, dst, t), sum_send.at[t, j], sum_recv.at[t, j], ctx, target * CORES + core)

    def second_stage(t):
        sum_copy(t, 0).wait_recv()
        keep = to(axes_of(t)[1])
        cut(part, keep, t)[...] = cut(part, keep, t)[...] + cut(landed, keep, t)[...]
        sum_copy(t, 2).start()

    kinds = (0, 1) if square else tuple(range(1, chips))
    for t in range(pieces):
        span = pl.ds(t * columns, columns)
        weight = jnp.concatenate([wo[p, :, span] for p in range(CORES)], axis=0)
        part[:, span] = product(attended, halves(weight))
        for j in kinds:
            sum_copy(t, j).start()
        if square and t >= 2:
            second_stage(t - 2)
    if square:
        for t in range(max(pieces - 2, 0), pieces):
            second_stage(t)
    for t in range(pieces):
        result = cut(part, chip, t)[...]
        if square:
            for j in (1, 2):
                sum_copy(t, j).wait_recv()
            result += cut(landed, chip, t)[...] + cut(landed, to(axes_of(t)[0]), t)[...]
        else:
            for j in kinds:
                sum_copy(t, j).wait_recv()
                result += cut(landed, origin(j), t)[...]
        out[:, pl.ds(t * columns, columns)] = result

    hid_drain()
    for t in range(pieces):
        for j in kinds + ((2,) if square else ()):
            sum_copy(t, j).wait_send()
    for d in range(ctx_n):
        @pl.when(d <= ctx)
        def _():
            @pl.when(ctx + 1 < ctx_n)
            def _():
                col_copy(ctx - d).wait_send()

            latents(ctx - d)[3]()
            twin_copy(ctx - d, core).wait_send()


def on_device(ctx_n, chips, hidden, w_query, w_down, latent_gain, w_key_up, w_value_up, w_out):
    rows, width = hidden.shape
    rank, nope = w_key_up.shape
    vdim = w_value_up.shape[1]
    per_core = chips * rows
    block = CORES * per_core
    lanes = -(-w_down.shape[1] // 128) * 128
    steps = 3 if width % 384 == 0 else 1
    square = chips == 4 and rows % 16 == 0 and width % 256 == 0
    pieces = 6 if width % 768 == 0 else 2
    f32, bf16, dma = jnp.float32, jnp.bfloat16, pltpu.SemaphoreType.DMA
    return pl.pallas_call(
        functools.partial(kernel, ctx_n, chips, square, steps, pieces),
        out_shape=jax.ShapeDtypeStruct((rows, width), f32),
        in_specs=[pl.BlockSpec(memory_space=pltpu.HBM)] * 7,
        out_specs=pl.BlockSpec(memory_space=pltpu.VMEM),
        scratch_shapes=[
            pltpu.VMEM((per_core, width), f32),
            pltpu.VMEM(w_down.shape[::-1], f32),
            pltpu.VMEM((CORES,) + w_query.shape[::-1], f32),
            pltpu.VMEM((1, rank), f32),
            pltpu.VMEM((CORES, rank, nope), f32),
            pltpu.VMEM((CORES, rank, vdim), f32),
            pltpu.VMEM((CORES, vdim, width), f32),
            pltpu.VMEM((ctx_n * block, lanes), f32),
            pltpu.VMEM((block, lanes), bf16),
            pltpu.VMEM((block, lanes), bf16),
            pltpu.VMEM((block, 1), f32),
            pltpu.VMEM((block, 1), f32),
            pltpu.VMEM((block, rank), f32),
            pltpu.VMEM((per_core, width), f32),
            pltpu.VMEM((per_core, width), f32),
            dma((2 + steps + 4,)),
            dma((4,)), dma((4,)),
            dma((chips, 2)), dma((chips, 2)),
            dma((ctx_n,)), dma((ctx_n,)),
            dma((ctx_n, chips, 2)), dma((ctx_n, chips, 2)),
            dma((ctx_n,)), dma((ctx_n,)),
            dma((pieces, chips)), dma((pieces, chips)),
        ],
        compiler_params=pltpu.CompilerParams(
            collective_id=0, has_side_effects=True, vmem_limit_bytes=60 * 1024 * 1024
        ),
    )(hidden, w_query.T, w_down.T, latent_gain.reshape(1, rank), w_key_up, w_value_up, w_out)


def solution(mesh):
    placed = (
        P(("ctx", "head"), None),
        P(None, "head"),
        P(),
        P(),
        P(None, "head"),
        P(None, "head"),
        P("head", None),
    )
    body = functools.partial(on_device, mesh.shape["ctx"], mesh.shape["head"] // CORES)
    return jax.shard_map(
        body, mesh=mesh, in_specs=placed, out_specs=P(("ctx", "head"), None), check_vma=False
    )
```

profile of v0, /device:TPU:24, one launch (start us, length us, event | category | flops | bytes accessed | tf_op | source)
XLA Modules:
  0.0 51.6 jit_solution(17369497597061734305)
XLA Ops:
  0.0 49.9 %shard_map.73 = f32[32,2304]{1,0:T(8,128)} custom-call(f32[32,2304]{1,0:T(8,128)} %hidden.1, f32[192,2304]{1,0:T(8,128)} %bitcast.4, f32[576,2304]{1,0:T(8,128)} %bitcast.3, f32[1,512]{1,0:T(1,128)} %bitcast.5, f32[512,128]{1,0:T(8,128)} %w_key.1, f32[512,128]{1,0:T(8,128)} %w_value.1, f32[128,2304]{1,0:T(8,128)} %w_out.1), custom_call_target="tpu_custom_call" | custom-call | tf_op jit(solution)/shard_map/pallas_call | solution.py:351
  49.9 1.7 %copy.9 = f32[32,2304]{1,0:T(8,128)} copy(f32[32,2304]{1,0:T(8,128)} %shard_map.73) | data formatting | bytes 589824
where the time goes:
time: 51.7 us; the launch traced here: 51.6 us
  Pallas kernels  49.9 us (97%)
  local copies, waits for them, and re-layouts  1.69 us (3%)
    pallas_call x1, Pallas kernels, on_device(): pl.pallas_call(functools.partial(kernel, ctx_n, chips, square, steps, pie...  49.9 us
    unnamed x1, local copies, waits for them, and re-layouts  1.69 us

commit v1 on v0

--- a/solution.py
+++ b/solution.py
@@ -10,6 +10,9 @@
 EPSILON = 1e-06
 FLOOR = -1e30
 CORES = 2
+LANE = 128
+DIRECT = ((1, 0), (2, 1), (1, 1), (2, 0))
+REST = ((1, 1), (2, 0), (3, 0), (3, 1))
 MESH = pl.DeviceIdType.MESH
 NN = (((1,), (0,)), ((), ()))
 NT = (((1,), (1,)), ((), ()))
@@ -26,7 +29,7 @@
     return dot(lh, rh) + (dot(ll, rh) + dot(lh, rl))
 
 
-def kernel(
+def general_kernel(
     ctx_n, chips, square, steps, pieces,
     hidden, w_query, w_down, gain, w_key, w_value, w_out, out,
     hid, wd, wq, gn, wk, wv, wo, lat, qh, ql, top, total, acc, part, landed,
@@ -337,6 +340,449 @@
             twin_copy(ctx - d, core).wait_send()
 
 
+def square_kernel(
+    ctx_n, chunks, cuts,
+    hidden, w_query, w_down, gain, w_key, w_value, w_out, out,
+    mine, hid, wd, gn, wq, wqh, wql, wk, wv, wo, woh, wol, lat, kh, kl, qh, ql, top, total, acc,
+    part, mid, fwd, near, last, res,
+    load_sem, out_sem, swap_send, swap_recv, hid_send, hid_recv, far_sem, z_send, z_recv,
+    lat_send, lat_recv, twin_send, twin_recv, sum_send, sum_recv,
+):
+    rows, width = hidden.shape
+    rank = gn.shape[1]
+    tail = wd.shape[0] - rank
+    nope, vdim = wk.shape[2], wv.shape[2]
+    key_width = wq.shape[1]
+    lanes = kh.shape[1]
+    r = rows // chunks
+    group = 4 * r
+    many = CORES * group
+    block = CORES * 4 * rows
+    hr = rows // 2
+    tiles = rank // LANE
+    piece = hr * tiles + hr // 2
+    slot = 2 * piece
+    half = width // 2
+    steps = 3 if width % 384 == 0 else 1
+    depth = width // steps
+    ctx = lax.axis_index("ctx")
+    head = lax.axis_index("head")
+    chip, core = head // CORES, head % CORES
+    twin = chip * CORES + (1 - core)
+    xbit, ybit = lax.rem(chip, 2), lax.div(chip, 2)
+    side = [None, (2 * ybit + 1 - xbit) * CORES + core, (2 * (1 - ybit) + xbit) * CORES + core]
+
+    def local(src, dst, sem):
+        return pltpu.make_async_copy(src, dst, sem)
+
+    def remote(src, dst, send, recv, h, c=ctx):
+        return pltpu.make_async_remote_copy(
+            src_ref=src, dst_ref=dst, send_sem=send, recv_sem=recv,
+            device_id={"ctx": c, "head": h}, device_id_type=MESH,
+        )
+
+    def signal(sem, c, h):
+        pl.semaphore_signal(sem, inc=1, device_id={"ctx": c, "head": h}, device_id_type=MESH)
+
+    def when(condition, *actions):
+        @pl.when(condition)
+        def _():
+            for action in actions:
+                action()
+
+    def spot(q, s, h):
+        return hid.at[pl.ds((q * 4 + s) * r, r), pl.ds(h * half, half)]
+
+    def hid_direct(q):
+        return [
+            remote(
+                hidden.at[pl.ds(q * r, r), pl.ds(h * half, half)], spot(q, a, h),
+                hid_send.at[q, a - 1, h], hid_recv.at[q, a - 1, h], side[a],
+            )
+            for a, h in DIRECT
+        ]
+
+    def hid_passed(q, h):
+        return remote(spot(q, 1 + h, h), spot(q, 3, h), hid_send.at[q, 2, h], hid_recv.at[q, 2, h], side[2 - h])
+
+    def hid_landed(q, s, h):
+        return remote(spot(q, s, h), spot(q, s, h), hid_send.at[q, s - 1, h], hid_recv.at[q, s - 1, h], twin)
+
+    def lat_at(d, p, s, h=0, size=piece):
+        return lat.at[pl.ds(((d * CORES + p) * 4 + s) * slot + h * piece, size)]
+
+    def lat_direct(d):
+        return [
+            remote(lat_at(d, 0, 0, h), lat_at(d, 0, a, h), lat_send.at[d, a - 1, h], lat_recv.at[d, a - 1, h], side[a])
+            for a, h in DIRECT
+        ]
+
+    def lat_passed(d, h):
+        return remote(
+            lat_at(d, 0, 1 + h, h), lat_at(d, 0, 3, h), lat_send.at[d, 2, h], lat_recv.at[d, 2, h], side[2 - h]
+        )
+
+    def lat_landed(d, s, h):
+        return remote(lat_at(d, 0, s, h), lat_at(d, 0, s, h), lat_send.at[d, s - 1, h], lat_recv.at[d, s - 1, h], twin)
+
+    def twin_own(d):
+        return remote(lat_at(d, 0, 0, 0, slot), lat_at(d, 1, 0, 0, slot), twin_send.at[d, 0], twin_recv.at[d, 0], twin)
+
+    def twin_rest(d):
+        size = 3 * slot
+        return remote(lat_at(d, 0, 1, 0, size), lat_at(d, 1, 1, 0, size), twin_send.at[d, 1], twin_recv.at[d, 1], twin)
+
+    def z_copy(d):
+        c = jnp.minimum(ctx + d, ctx_n - 1)
+        return remote(lat_at(0, 0, 0, 0, slot), lat_at(d, 0, 0, 0, slot), z_send.at[d], z_recv.at[d], head, c)
+
+    def lat_spread(d):
+        for copy in lat_direct(d):
+            copy.start()
+        twin_own(d).start()
+
+    def lat_fetch(d):
+        z_copy(d).wait_recv()
+        lat_spread(d)
+
+    def lat_relay(d):
+        for h in range(2):
+            lat_landed(d, 1 + h, h).wait_recv()
+            lat_passed(d, h).start()
+
+    def lat_finish(d):
+        for s, h in REST:
+            lat_landed(d, s, h).wait_recv()
+        twin_rest(d).start()
+
+    def hid_relay(q):
+        for h in range(2):
+            hid_landed(q, 1 + h, h).wait_recv()
+            hid_passed(q, h).start()
+
+    def hid_finish(q):
+        for s, h in REST:
+            hid_landed(q, s, h).wait_recv()
+
+    loads = [local(hidden, mine, load_sem.at[0]), local(gain, gn, load_sem.at[1])]
+    for i in range(steps):
+        span = pl.ds(i * depth, depth)
+        loads.append(local(w_down.at[:, span], wd.at[:, span], load_sem.at[2 + i]))
+    pairs = [(w_query, wq), (w_key, wk), (w_value, wv), (w_out, wo)]
+    own = [local(src, dst.at[0], load_sem.at[2 + steps + i]) for i, (src, dst) in enumerate(pairs)]
+    for q in range(chunks):
+        own.append(
+            local(hidden.at[pl.ds(q * r, r)], hid.at[pl.ds(q * group, r)], load_sem.at[2 + steps + len(pairs) + q])
+        )
+    for copy in loads:
+        copy.start()
+
+    barrier = pltpu.get_barrier_semaphore()
+    for h in (twin, side[1], side[2]):
+        signal(barrier, ctx, h)
+    when(ctx > 0, lambda: signal(barrier, ctx - 1, head))
+    when(ctx + 1 < ctx_n, lambda: signal(barrier, ctx + 1, head))
+    pl.semaphore_wait(barrier, 3 + jnp.minimum(ctx, 1) + jnp.minimum(ctx_n - 1 - ctx, 1))
+
+    for copy in hid_direct(0):
+        copy.start()
+    swaps = [remote(src, dst.at[1], swap_send.at[i], swap_recv.at[i], twin) for i, (src, dst) in enumerate(pairs)]
+    for copy in own:
+        copy.start()
+    for copy in swaps:
+        copy.start()
+
+    if ctx_n > 2:
+        when(jnp.logical_and(ctx >= 1, ctx + 2 <= ctx_n), lambda: signal(far_sem.at[2], ctx - 1, head))
+
+    loads[0].wait()
+    loads[1].wait()
+    down = jnp.zeros((rows, rank + tail), jnp.float32)
+    for i in range(steps):
+        loads[2 + i].wait()
+        span = pl.ds(i * depth, depth)
+        down += product(halves(mine[:, span]), halves(wd[:, span]), NT)
+    raw = down[:, :rank]
+    meansq = jnp.mean(raw * raw, axis=-1, keepdims=True)
+    latent = raw * lax.rsqrt(meansq + EPSILON) * gn[...]
+    shared = jnp.concatenate([down[:hr, rank:], down[hr:, rank:]], axis=1)
+    for h in range(2):
+        for j in range(tiles):
+            lat_at(0, 0, 0, h)[pl.ds(j * hr, hr), :] = latent[h * hr : (h + 1) * hr, j * LANE : (j + 1) * LANE]
+        lat_at(0, 0, 0, h)[pl.ds(tiles * hr, hr // 2), :] = shared[h * hr // 2 : (h + 1) * hr // 2]
+
+    for d in range(2, ctx_n):
+        when(ctx + d < ctx_n, lambda d=d: pl.semaphore_wait(far_sem.at[d], 1))
+        if d + 1 < ctx_n:
+            when(
+                jnp.logical_and(ctx >= 1, ctx + d < ctx_n),
+                lambda d=d: signal(far_sem.at[d + 1], ctx - 1, head),
+            )
+    for d in range(ctx_n - 1, 0, -1):
+        when(ctx + d < ctx_n, lambda d=d: z_copy(d).start())
+    lat_spread(0)
+
+    def split_query(p):
+        wqh[p], wql[p] = halves(wq[p])
+
+    hid_relay(0)
+    own[0].wait()
+    split_query(0)
+    lat_relay(0)
+    if ctx_n > 1:
+        when(ctx >= 1, lambda: lat_fetch(1))
+    for i in range(2):
+        swaps[i].wait()
+    own[1].wait()
+    split_query(1)
+
+    scale = key_width ** (-0.5)
+    pad = jnp.zeros((group, lanes - rank - tail), jnp.float32)
+
+    def queries(q):
+        own[len(pairs) + q].wait()
+        hid_finish(q)
+        query = [jnp.zeros((group, key_width), jnp.float32) for _ in range(CORES)]
+        for i in range(steps):
+            span = pl.ds(i * depth, depth)
+            given = halves(hid[pl.ds(q * group, group), span])
+            for p in range(CORES):
+                query[p] += product(given, (wqh[p, :, span], wql[p, :, span]), NT)
+        for p in range(CORES):
+            wide = product(halves(query[p][:, :nope] * scale), halves(wk[p]), NT)
+            span = pl.ds(q * many + p * group, group)
+            qh[span, :rank], ql[span, :rank] = halves(wide)
+            rest = jnp.concatenate([query[p][:, nope:] * scale, pad], axis=1)
+            qh[span, rank:], ql[span, rank:] = halves(rest)
+
+    def keys(d):
+        for p in range(CORES):
+            for s in range(4):
+                at = d * block + (p * 4 + s) * rows
+                packed = jnp.concatenate(
+                    [lat_at(d, p, s, h)[pl.ds(tiles * hr, hr // 2), :] for h in range(2)], axis=0
+                )
+                for h in range(2):
+                    span = pl.ds(at + h * hr, hr)
+                    for j in range(tiles):
+                        lane = pl.ds(j * LANE, LANE)
+                        kh[span, lane], kl[span, lane] = halves(lat_at(d, p, s, h)[pl.ds(j * hr, hr), :])
+                    lane = pl.ds(rank, LANE)
+                    kh[span, lane], kl[span, lane] = halves(packed if h == 0 else pltpu.roll(packed, tail, 1))
+
+    def lat_ready(d):
+        twin_own(d).wait_recv()
+        twin_rest(d).wait_recv()
+        keys(d)
+
+    def place(s, parity, i):
+        sx, sy = lax.rem(s, 2), lax.div(s, 2)
+        x, y = lax.rem(xbit + sx, 2), lax.rem(ybit + sy, 2)
+        return ((2 * y + x) * CORES + parity) * rows + i
+
+    def attend(q, d):
+        mine_q = pl.ds(q * many, many)
+        those = pl.ds(d * block, block)
+        scores = product((qh[mine_q, :], ql[mine_q, :]), (kh[those, :], kl[those, :]), NT)
+        if d == 0:
+            line = lax.rem(lax.broadcasted_iota(jnp.int32, (many, 1), 0), group)
+            column = lax.broadcasted_iota(jnp.int32, (1, block), 1)
+            there = lax.div(column, 4 * rows)
+            column = lax.rem(column, 4 * rows)
+            asked = place(lax.div(line, r), core, q * r + lax.rem(line, r))
+            held = place(lax.div(column, rows), core + there - 2 * core * there, lax.rem(column, rows))
+            causal = asked >= held
+            scores = jnp.where(causal, scores, FLOOR)
+            peak = jnp.max(scores, axis=1, keepdims=True)
+        else:
+            peak = jnp.maximum(top[mine_q, :], jnp.max(scores, axis=1, keepdims=True))
+        weights = jnp.exp(scores - peak)
+        if d == 0:
+            weights = jnp.where(causal, weights, 0.0)
+        mixed = product(halves(weights), (kh[those, :rank], kl[those, :rank]))
+        added = jnp.sum(weights, axis=1, keepdims=True)
+        if d == 0:
+            total[mine_q, :] = added
+            acc[mine_q, :] = mixed
+        else:
+            fade = jnp.exp(top[mine_q, :] - peak)
+            total[mine_q, :] = total[mine_q, :] * fade + added
+            acc[mine_q, :] = acc[mine_q, :] * fade + mixed
+        top[mine_q, :] = peak
+
+    def span_of(q, t):
+        columns = width // cuts[q]
+        return pl.ds(t * columns, columns)
+
+    def axes_of(t):
+        return (1, 2) if t % 2 == 0 else (2, 1)
+
+    def sum_copy(q, t, j):
+        first, second = axes_of(t)
+        span = span_of(q, t)
+        here = pl.ds(q * r, r)
+
+        def part_of(s):
+            return part.at[pl.ds(q * group + s * r, r), span]
+
+        src, dst, target = [
+            (part_of(3), mid.at[here, span], first),
+            (part_of(first), near.at[here, span], first),
+            (fwd.at[here, span], last.at[here, span], second),
+        ][j]
+        return remote(src, dst, sum_send.at[q, t, j], sum_recv.at[q, t, j], side[target])
+
+    def project(q):
+        found = []
+        for p in range(CORES):
+            span = pl.ds(q * many + p * group, group)
+            found.append(product(halves(acc[span, :] / total[span, :]), halves(wv[p])))
+        attended = halves(jnp.concatenate(found, axis=1))
+        for t in range(cuts[q]):
+            span = span_of(q, t)
+            part[pl.ds(q * group, group), span] = product(attended, (woh[:, span], wol[:, span]))
+            for j in range(2):
+                sum_copy(q, t, j).start()
+
+    def second_stage(q):
+        here = pl.ds(q * r, r)
+        for t in range(cuts[q]):
+            span = span_of(q, t)
+            sum_copy(q, t, 0).wait_recv()
+            keep = axes_of(t)[1]
+            fwd[here, span] = part[pl.ds(q * group + keep * r, r), span] + mid[here, span]
+            sum_copy(q, t, 2).start()
+
+    def out_copy(q, t):
+        here, span = pl.ds(q * r, r), span_of(q, t)
+        return local(res.at[here, span], out.at[here, span], out_sem.at[q, t])
+
+    def collect(q):
+        here = pl.ds(q * r, r)
+        for t in range(cuts[q]):
+            span = span_of(q, t)
+            for j in (1, 2):
+                sum_copy(q, t, j).wait_recv()
+            res[here, span] = part[pl.ds(q * group, r), span] + near[here, span] + last[here, span]
+            out_copy(q, t).start()
+
+    def attend_all(q, ready):
+        for d in range(1, ctx_n):
+            def step(d=d):
+                if ready:
+                    lat_finish(d)
+                    lat_ready(d)
+                attend(q, d)
+
+            when(d <= ctx, step)
+
+    def split_out():
+        for i in range(2, len(pairs)):
+            own[i].wait()
+            swaps[i].wait()
+        for p in range(CORES):
+            span = pl.ds(p * vdim, vdim)
+            woh[span, :], wol[span, :] = halves(wo[p])
+
+    queries(0)
+    if ctx_n > 2:
+        when(ctx >= 2, lambda: lat_fetch(2))
+    if ctx_n > 1:
+        when(ctx >= 1, lambda: lat_relay(1))
+    for d in range(3, ctx_n):
+        when(ctx >= d, lambda d=d: lat_fetch(d))
+    lat_finish(0)
+    split_out()
+    lat_ready(0)
+    attend(0, 0)
+    for d in range(2, ctx_n):
+        when(ctx >= d, lambda d=d: lat_relay(d))
+    for q in range(1, chunks):
+        for copy in hid_direct(q):
+            copy.start()
+    attend_all(0, True)
+    for q in range(1, chunks):
+        hid_relay(q)
+    project(0)
+    for q in range(1, chunks):
+        queries(q)
+        second_stage(q - 1)
+        attend(q, 0)
+        attend_all(q, False)
+        project(q)
+        collect(q - 1)
+    second_stage(chunks - 1)
+    collect(chunks - 1)
+
+    for q in range(chunks):
+        for copy in hid_direct(q) + [hid_passed(q, h) for h in range(2)]:
+            copy.wait_send()
+        for t in range(cuts[q]):
+            for j in range(3):
+                sum_copy(q, t, j).wait_send()
+            out_copy(q, t).wait()
+    for d in range(ctx_n):
+        def drain(d=d):
+            for copy in lat_direct(d) + [lat_passed(d, h) for h in range(2)] + [twin_own(d), twin_rest(d)]:
+                copy.wait_send()
+
+        when(d <= ctx, drain)
+        if d > 0:
+            when(ctx + d < ctx_n, lambda d=d: z_copy(d).wait_send())
+
+
+def square_call(ctx_n, hidden, w_query, w_down, gain, w_key_up, w_value_up, w_out):
+    rows, width = hidden.shape
+    rank, nope = w_key_up.shape
+    vdim = w_value_up.shape[1]
+    f32, bf16, dma = jnp.float32, jnp.bfloat16, pltpu.SemaphoreType.DMA
+    chunks = 2
+    cuts = (2, 6)
+    r = rows // chunks
+    block = CORES * 4 * rows
+    lanes = rank + LANE
+    steps = 3 if width % 384 == 0 else 1
+    slot = rows * (rank // LANE) + rows // 2
+    query = (CORES,) + w_query.shape
+    both = (CORES * vdim, width)
+    return pl.pallas_call(
+        functools.partial(square_kernel, ctx_n, chunks, cuts),
+        out_shape=jax.ShapeDtypeStruct((rows, width), f32),
+        in_specs=[pl.BlockSpec(memory_space=pltpu.HBM)] * 7,
+        out_specs=pl.BlockSpec(memory_space=pltpu.HBM),
+        scratch_shapes=[
+            pltpu.VMEM((rows, width), f32),
+            pltpu.VMEM((4 * rows, width), f32),
+            pltpu.VMEM(w_down.shape, f32),
+            pltpu.VMEM((1, rank), f32),
+            pltpu.VMEM(query, f32), pltpu.VMEM(query, bf16), pltpu.VMEM(query, bf16),
+            pltpu.VMEM((CORES, rank, nope), f32),
+            pltpu.VMEM((CORES, rank, vdim), f32),
+            pltpu.VMEM((CORES, vdim, width), f32), pltpu.VMEM(both, bf16), pltpu.VMEM(both, bf16),
+            pltpu.VMEM((ctx_n * CORES * 4 * slot, LANE), f32),
+            pltpu.VMEM((ctx_n * block, lanes), bf16), pltpu.VMEM((ctx_n * block, lanes), bf16),
+            pltpu.VMEM((block, lanes), bf16), pltpu.VMEM((block, lanes), bf16),
+            pltpu.VMEM((block, 1), f32),
+            pltpu.VMEM((block, 1), f32),
+            pltpu.VMEM((block, rank), f32),
+            pltpu.VMEM((4 * rows, width), f32),
+        ] + [pltpu.VMEM((rows, width), f32)] * 5 + [
+            dma((2 + steps + 4 + chunks,)),
+            dma((chunks, max(cuts))),
+            dma((4,)), dma((4,)),
+            dma((chunks, 3, 2)), dma((chunks, 3, 2)),
+            pltpu.SemaphoreType.REGULAR((ctx_n,)),
+            dma((ctx_n,)), dma((ctx_n,)),
+            dma((ctx_n, 3, 2)), dma((ctx_n, 3, 2)),
+            dma((ctx_n, 2)), dma((ctx_n, 2)),
+            dma((chunks, max(cuts), 3)), dma((chunks, max(cuts), 3)),
+        ],
+        compiler_params=pltpu.CompilerParams(
+            collective_id=0, has_side_effects=True, vmem_limit_bytes=60 * 1024 * 1024
+        ),
+    )(hidden, w_query, w_down, gain, w_key_up, w_value_up, w_out)
+
+
 def on_device(ctx_n, chips, hidden, w_query, w_down, latent_gain, w_key_up, w_value_up, w_out):
     rows, width = hidden.shape
     rank, nope = w_key_up.shape
@@ -345,11 +791,15 @@
     block = CORES * per_core
     lanes = -(-w_down.shape[1] // 128) * 128
     steps = 3 if width % 384 == 0 else 1
+    if chips == 4 and rows % 32 == 0 and width % 768 == 0 and rank % LANE == 0 and 2 * (w_down.shape[1] - rank) == LANE:
+        return square_call(
+            ctx_n, hidden, w_query.T, w_down.T, latent_gain.reshape(1, rank), w_key_up, w_value_up, w_out
+        )
     square = chips == 4 and rows % 16 == 0 and width % 256 == 0
     pieces = 6 if width % 768 == 0 else 2
     f32, bf16, dma = jnp.float32, jnp.bfloat16, pltpu.SemaphoreType.DMA
     return pl.pallas_call(
-        functools.partial(kernel, ctx_n, chips, square, steps, pieces),
+        functools.partial(general_kernel, ctx_n, chips, square, steps, pieces),
         out_shape=jax.ShapeDtypeStruct((rows, width), f32),
         in_specs=[pl.BlockSpec(memory_space=pltpu.HBM)] * 7,
         out_specs=pl.BlockSpec(memory_space=pltpu.VMEM),

time: 51.7 us -> 48 us (0.928)
  Pallas kernels: 49.9 us -> 46.1 us
    pallas_call x1, Pallas kernels: 49.9 us -> 46.1 us  [square_call(): pl.pallas_call(functools.partial(square_kernel, ctx_n, chunks, cuts), out...]
where the time goes in v1:
time: 48 us; the launch traced here: 47.8 us
  Pallas kernels  46.1 us (96%)
  local copies, waits for them, and re-layouts  1.69 us (4%)
    pallas_call x1, Pallas kernels, square_call(): pl.pallas_call(functools.partial(square_kernel, ctx_n, chunks, cuts), out...  46.1 us
    unnamed x1, local copies, waits for them, and re-layouts  1.69 us

profile of v1, /device:TPU:24, one launch (start us, length us, event | category | flops | bytes accessed | tf_op | source)
XLA Modules:
  0.0 47.8 jit_solution(15038837169036913138)
XLA Ops:
  0.0 46.1 %shard_map.73 = f32[32,2304]{1,0:T(8,128)} custom-call(f32[32,2304]{1,0:T(8,128)} %hidden.1, f32[192,2304]{1,0:T(8,128)} %bitcast.4, f32[576,2304]{1,0:T(8,128)} %bitcast.3, f32[1,512]{1,0:T(1,128)} %bitcast.5, f32[512,128]{1,0:T(8,128)} %w_key.1, f32[512,128]{1,0:T(8,128)} %w_value.1, f32[128,2304]{1,0:T(8,128)} %w_out.1), custom_call_target="tpu_custom_call" | custom-call | tf_op jit(solution)/shard_map/pallas_call | solution.py:748
  46.1 1.7 %copy.9 = f32[32,2304]{1,0:T(8,128)} copy(f32[32,2304]{1,0:T(8,128)} %shard_map.73) | data formatting | bytes 589824

commit v2 on v1

--- a/solution.py
+++ b/solution.py
@@ -11,6 +11,7 @@
 FLOOR = -1e30
 CORES = 2
 LANE = 128
+FIRST = ((1, 0), (2, 1))
 DIRECT = ((1, 0), (2, 1), (1, 1), (2, 0))
 REST = ((1, 1), (2, 0), (3, 0), (3, 1))
 MESH = pl.DeviceIdType.MESH
@@ -27,6 +28,14 @@
     (lh, ll), (rh, rl) = left, right
     dot = functools.partial(lax.dot_general, dimension_numbers=dims, preferred_element_type=jnp.float32)
     return dot(lh, rh) + (dot(ll, rh) + dot(lh, rl))
+
+
+def stacked(left, right, dims=NN):
+    (lh, ll), (rh, rl) = left, right
+    dot = functools.partial(lax.dot_general, dimension_numbers=dims, preferred_element_type=jnp.float32)
+    both = dot(jnp.concatenate([lh, ll], axis=0), rh)
+    size = lh.shape[0]
+    return both[:size] + (both[size:] + dot(lh, rl))
 
 
 def general_kernel(
@@ -346,7 +355,7 @@
     mine, hid, wd, gn, wq, wqh, wql, wk, wv, wo, woh, wol, lat, kh, kl, qh, ql, top, total, acc,
     part, mid, fwd, near, last, res,
     load_sem, out_sem, swap_send, swap_recv, hid_send, hid_recv, far_sem, z_send, z_recv,
-    lat_send, lat_recv, twin_send, twin_recv, sum_send, sum_recv,
+    lat_send, lat_recv, twin_recv, sum_send, sum_recv,
 ):
     rows, width = hidden.shape
     rank = gn.shape[1]
@@ -393,87 +402,79 @@
     def spot(q, s, h):
         return hid.at[pl.ds((q * 4 + s) * r, r), pl.ds(h * half, half)]
 
-    def hid_direct(q):
-        return [
+    def hid_direct(q, order):
+        for a, h in order:
             remote(
                 hidden.at[pl.ds(q * r, r), pl.ds(h * half, half)], spot(q, a, h),
-                hid_send.at[q, a - 1, h], hid_recv.at[q, a - 1, h], side[a],
-            )
-            for a, h in DIRECT
-        ]
-
-    def hid_passed(q, h):
-        return remote(spot(q, 1 + h, h), spot(q, 3, h), hid_send.at[q, 2, h], hid_recv.at[q, 2, h], side[2 - h])
-
-    def hid_landed(q, s, h):
-        return remote(spot(q, s, h), spot(q, s, h), hid_send.at[q, s - 1, h], hid_recv.at[q, s - 1, h], twin)
+                hid_send.at[0], hid_recv.at[q, h if (a, h) in FIRST else 2], side[a],
+            ).start()
+
+    def hid_relay(q):
+        for h in range(2):
+            landed = spot(q, 1 + h, h)
+            remote(landed, landed, hid_send.at[0], hid_recv.at[q, h], twin).wait_recv()
+            remote(landed, spot(q, 3, h), hid_send.at[0], hid_recv.at[q, 2], side[2 - h]).start()
+
+    def hid_finish(q):
+        landed = hid.at[pl.ds((q * 4 + 1) * r, 2 * r)]
+        remote(landed, landed, hid_send.at[0], hid_recv.at[q, 2], twin).wait_recv()
 
     def lat_at(d, p, s, h=0, size=piece):
         return lat.at[pl.ds(((d * CORES + p) * 4 + s) * slot + h * piece, size)]
 
-    def lat_direct(d):
-        return [
-            remote(lat_at(d, 0, 0, h), lat_at(d, 0, a, h), lat_send.at[d, a - 1, h], lat_recv.at[d, a - 1, h], side[a])
-            for a, h in DIRECT
-        ]
-
-    def lat_passed(d, h):
-        return remote(
-            lat_at(d, 0, 1 + h, h), lat_at(d, 0, 3, h), lat_send.at[d, 2, h], lat_recv.at[d, 2, h], side[2 - h]
-        )
-
-    def lat_landed(d, s, h):
-        return remote(lat_at(d, 0, s, h), lat_at(d, 0, s, h), lat_send.at[d, s - 1, h], lat_recv.at[d, s - 1, h], twin)
-
-    def twin_own(d):
-        return remote(lat_at(d, 0, 0, 0, slot), lat_at(d, 1, 0, 0, slot), twin_send.at[d, 0], twin_recv.at[d, 0], twin)
-
-    def twin_rest(d):
-        size = 3 * slot
-        return remote(lat_at(d, 0, 1, 0, size), lat_at(d, 1, 1, 0, size), twin_send.at[d, 1], twin_recv.at[d, 1], twin)
-
-    def z_copy(d):
+    def lat_twin(d, s, count):
+        size = count * slot
+        remote(lat_at(d, 0, s, 0, size), lat_at(d, 1, s, 0, size), lat_send.at[d], twin_recv.at[d], twin).start()
+
+    def z_copy(d, s, h, size):
         c = jnp.minimum(ctx + d, ctx_n - 1)
-        return remote(lat_at(0, 0, 0, 0, slot), lat_at(d, 0, 0, 0, slot), z_send.at[d], z_recv.at[d], head, c)
+        return remote(lat_at(0, 0, s, h, size), lat_at(d, 0, s, h, size), z_send.at[d - 1], z_recv.at[d - 1], head, c)
+
+    def z_wait(d):
+        landed = lat_at(d, 0, 0, 0, 4 * slot if d == 1 else slot)
+        remote(landed, landed, z_send.at[d - 1], z_recv.at[d - 1], head).wait_recv()
 
     def lat_spread(d):
-        for copy in lat_direct(d):
-            copy.start()
-        twin_own(d).start()
+        for a, h in DIRECT:
+            remote(
+                lat_at(d, 0, 0, h), lat_at(d, 0, a, h), lat_send.at[d],
+                lat_recv.at[d, h if (a, h) in FIRST else 2], side[a],
+            ).start()
+        lat_twin(d, 0, 1)
 
     def lat_fetch(d):
-        z_copy(d).wait_recv()
+        z_wait(d)
         lat_spread(d)
 
     def lat_relay(d):
         for h in range(2):
-            lat_landed(d, 1 + h, h).wait_recv()
-            lat_passed(d, h).start()
+            landed = lat_at(d, 0, 1 + h, h)
+            remote(landed, landed, lat_send.at[d], lat_recv.at[d, h], twin).wait_recv()
+            remote(landed, lat_at(d, 0, 3, h), lat_send.at[d], lat_recv.at[d, 2], side[2 - h]).start()
 
     def lat_finish(d):
-        for s, h in REST:
-            lat_landed(d, s, h).wait_recv()
-        twin_rest(d).start()
-
-    def hid_relay(q):
-        for h in range(2):
-            hid_landed(q, 1 + h, h).wait_recv()
-            hid_passed(q, h).start()
-
-    def hid_finish(q):
-        for s, h in REST:
-            hid_landed(q, s, h).wait_recv()
+        landed = lat_at(d, 0, 1, 0, 2 * slot)
+        remote(landed, landed, lat_send.at[d], lat_recv.at[d, 2], twin).wait_recv()
+        lat_twin(d, 1, 3)
+
+    def z_begin():
+        z_copy(1, 0, 0, slot).start()
+        z_copy(1, 1, 0, piece).start()
+        z_copy(1, 2, 1, piece).start()
+
+    def z_end():
+        z_copy(1, 1, 1, 2 * piece).start()
+        z_copy(1, 3, 0, slot).start()
 
     loads = [local(hidden, mine, load_sem.at[0]), local(gain, gn, load_sem.at[1])]
     for i in range(steps):
         span = pl.ds(i * depth, depth)
         loads.append(local(w_down.at[:, span], wd.at[:, span], load_sem.at[2 + i]))
     pairs = [(w_query, wq), (w_key, wk), (w_value, wv), (w_out, wo)]
-    own = [local(src, dst.at[0], load_sem.at[2 + steps + i]) for i, (src, dst) in enumerate(pairs)]
+    lots = (0, 1, 1, 2)
+    own = [local(src, dst.at[0], load_sem.at[2 + steps + lot]) for (src, dst), lot in zip(pairs, lots)]
     for q in range(chunks):
-        own.append(
-            local(hidden.at[pl.ds(q * r, r)], hid.at[pl.ds(q * group, r)], load_sem.at[2 + steps + len(pairs) + q])
-        )
+        own.append(local(hidden.at[pl.ds(q * r, r)], hid.at[pl.ds(q * group, r)], load_sem.at[5 + steps]))
     for copy in loads:
         copy.start()
 
@@ -484,16 +485,17 @@
     when(ctx + 1 < ctx_n, lambda: signal(barrier, ctx + 1, head))
     pl.semaphore_wait(barrier, 3 + jnp.minimum(ctx, 1) + jnp.minimum(ctx_n - 1 - ctx, 1))
 
-    for copy in hid_direct(0):
-        copy.start()
-    swaps = [remote(src, dst.at[1], swap_send.at[i], swap_recv.at[i], twin) for i, (src, dst) in enumerate(pairs)]
+    hid_direct(0, FIRST + REST[:2])
+    swaps = [
+        remote(src, dst.at[1], swap_send.at[lot], swap_recv.at[lot], twin) for (src, dst), lot in zip(pairs, lots)
+    ]
     for copy in own:
         copy.start()
     for copy in swaps:
         copy.start()
 
     if ctx_n > 2:
-        when(jnp.logical_and(ctx >= 1, ctx + 2 <= ctx_n), lambda: signal(far_sem.at[2], ctx - 1, head))
+        when(jnp.logical_and(ctx >= 1, ctx + 2 <= ctx_n), lambda: signal(far_sem.at[0], ctx - 1, head))
 
     loads[0].wait()
     loads[1].wait()
@@ -501,7 +503,7 @@
     for i in range(steps):
         loads[2 + i].wait()
         span = pl.ds(i * depth, depth)
-        down += product(halves(mine[:, span]), halves(wd[:, span]), NT)
+        down += stacked(halves(mine[:, span]), halves(wd[:, span]), NT)
     raw = down[:, :rank]
     meansq = jnp.mean(raw * raw, axis=-1, keepdims=True)
     latent = raw * lax.rsqrt(meansq + EPSILON) * gn[...]
@@ -512,44 +514,55 @@
         lat_at(0, 0, 0, h)[pl.ds(tiles * hr, hr // 2), :] = shared[h * hr // 2 : (h + 1) * hr // 2]
 
     for d in range(2, ctx_n):
-        when(ctx + d < ctx_n, lambda d=d: pl.semaphore_wait(far_sem.at[d], 1))
+        when(ctx + d < ctx_n, lambda d=d: pl.semaphore_wait(far_sem.at[d - 2], 1))
         if d + 1 < ctx_n:
             when(
                 jnp.logical_and(ctx >= 1, ctx + d < ctx_n),
-                lambda d=d: signal(far_sem.at[d + 1], ctx - 1, head),
+                lambda d=d: signal(far_sem.at[d - 1], ctx - 1, head),
             )
-    for d in range(ctx_n - 1, 0, -1):
-        when(ctx + d < ctx_n, lambda d=d: z_copy(d).start())
+    for d in range(ctx_n - 1, 1, -1):
+        when(ctx + d < ctx_n, lambda d=d: z_copy(d, 0, 0, slot).start())
     lat_spread(0)
 
     def split_query(p):
         wqh[p], wql[p] = halves(wq[p])
+
+    def kept(lot):
+        whole = {0: wq.at[0], 1: wk, 2: wo.at[0]}[lot]
+        local(whole, whole, load_sem.at[2 + steps + lot]).wait()
+        remote(whole, whole, swap_send.at[lot], swap_recv.at[lot], twin).wait()
 
     hid_relay(0)
     own[0].wait()
     split_query(0)
     lat_relay(0)
     if ctx_n > 1:
-        when(ctx >= 1, lambda: lat_fetch(1))
-    for i in range(2):
-        swaps[i].wait()
-    own[1].wait()
+        when(ctx + 1 < ctx_n, z_begin)
+    for q in range(1, chunks):
+        hid_direct(q, FIRST)
+    swaps[0].wait()
     split_query(1)
+    for d in range(2, ctx_n):
+        when(ctx >= d, lambda d=d: lat_fetch(d))
+    lat_finish(0)
+    if ctx_n > 1:
+        when(ctx + 1 < ctx_n, z_end)
+    kept(1)
+    local(mine, mine, load_sem.at[5 + steps]).wait()
 
     scale = key_width ** (-0.5)
     pad = jnp.zeros((group, lanes - rank - tail), jnp.float32)
 
     def queries(q):
-        own[len(pairs) + q].wait()
         hid_finish(q)
         query = [jnp.zeros((group, key_width), jnp.float32) for _ in range(CORES)]
         for i in range(steps):
             span = pl.ds(i * depth, depth)
             given = halves(hid[pl.ds(q * group, group), span])
             for p in range(CORES):
-                query[p] += product(given, (wqh[p, :, span], wql[p, :, span]), NT)
+                query[p] += stacked(given, (wqh[p, :, span], wql[p, :, span]), NT)
         for p in range(CORES):
-            wide = product(halves(query[p][:, :nope] * scale), halves(wk[p]), NT)
+            wide = stacked(halves(query[p][:, :nope] * scale), halves(wk[p]), NT)
             span = pl.ds(q * many + p * group, group)
             qh[span, :rank], ql[span, :rank] = halves(wide)
             rest = jnp.concatenate([query[p][:, nope:] * scale, pad], axis=1)
@@ -571,8 +584,8 @@
                     kh[span, lane], kl[span, lane] = halves(packed if h == 0 else pltpu.roll(packed, tail, 1))
 
     def lat_ready(d):
-        twin_own(d).wait_recv()
-        twin_rest(d).wait_recv()
+        landed = lat_at(d, 1, 0, 0, 4 * slot)
+        remote(landed, landed, lat_send.at[d], twin_recv.at[d], twin).wait_recv()
         keys(d)
 
     def place(s, parity, i):
@@ -583,7 +596,7 @@
     def attend(q, d):
         mine_q = pl.ds(q * many, many)
         those = pl.ds(d * block, block)
-        scores = product((qh[mine_q, :], ql[mine_q, :]), (kh[those, :], kl[those, :]), NT)
+        scores = stacked((qh[mine_q, :], ql[mine_q, :]), (kh[those, :], kl[those, :]), NT)
         if d == 0:
             line = lax.rem(lax.broadcasted_iota(jnp.int32, (many, 1), 0), group)
             column = lax.broadcasted_iota(jnp.int32, (1, block), 1)
@@ -599,7 +612,7 @@
         weights = jnp.exp(scores - peak)
         if d == 0:
             weights = jnp.where(causal, weights, 0.0)
-        mixed = product(halves(weights), (kh[those, :rank], kl[those, :rank]))
+        mixed = stacked(halves(weights), (kh[those, :rank], kl[those, :rank]))
         added = jnp.sum(weights, axis=1, keepdims=True)
         if d == 0:
             total[mine_q, :] = added
@@ -630,17 +643,17 @@
             (part_of(first), near.at[here, span], first),
             (fwd.at[here, span], last.at[here, span], second),
         ][j]
-        return remote(src, dst, sum_send.at[q, t, j], sum_recv.at[q, t, j], side[target])
+        return remote(src, dst, sum_send.at[0], sum_recv.at[sum(cuts[:q]) + t, min(j, 1)], side[target])
 
     def project(q):
         found = []
         for p in range(CORES):
             span = pl.ds(q * many + p * group, group)
-            found.append(product(halves(acc[span, :] / total[span, :]), halves(wv[p])))
+            found.append(stacked(halves(acc[span, :] / total[span, :]), halves(wv[p])))
         attended = halves(jnp.concatenate(found, axis=1))
         for t in range(cuts[q]):
             span = span_of(q, t)
-            part[pl.ds(q * group, group), span] = product(attended, (woh[:, span], wol[:, span]))
+            part[pl.ds(q * group, group), span] = stacked(attended, (woh[:, span], wol[:, span]))
             for j in range(2):
                 sum_copy(q, t, j).start()
 
@@ -655,80 +668,78 @@
 
     def out_copy(q, t):
         here, span = pl.ds(q * r, r), span_of(q, t)
-        return local(res.at[here, span], out.at[here, span], out_sem.at[q, t])
+        return local(res.at[here, span], out.at[here, span], out_sem.at[0])
 
     def collect(q):
         here = pl.ds(q * r, r)
         for t in range(cuts[q]):
             span = span_of(q, t)
-            for j in (1, 2):
-                sum_copy(q, t, j).wait_recv()
+            landed = near.at[pl.ds(0, 2 * r), span]
+            remote(landed, landed, sum_send.at[0], sum_recv.at[sum(cuts[:q]) + t, 1], twin).wait_recv()
             res[here, span] = part[pl.ds(q * group, r), span] + near[here, span] + last[here, span]
             out_copy(q, t).start()
 
-    def attend_all(q, ready):
-        for d in range(1, ctx_n):
-            def step(d=d):
-                if ready:
-                    lat_finish(d)
-                    lat_ready(d)
-                attend(q, d)
-
-            when(d <= ctx, step)
+    def attend_late(q, d, ready):
+        def step():
+            if ready and d == 1:
+                z_wait(1)
+                lat_twin(1, 0, 4)
+            elif ready:
+                lat_finish(d)
+            if ready:
+                lat_ready(d)
+            attend(q, d)
+
+        when(d <= ctx, step)
 
     def split_out():
-        for i in range(2, len(pairs)):
-            own[i].wait()
-            swaps[i].wait()
+        kept(2)
         for p in range(CORES):
             span = pl.ds(p * vdim, vdim)
             woh[span, :], wol[span, :] = halves(wo[p])
 
+    late = list(range(2, ctx_n)) + [1] * (ctx_n > 1)
     queries(0)
-    if ctx_n > 2:
-        when(ctx >= 2, lambda: lat_fetch(2))
-    if ctx_n > 1:
-        when(ctx >= 1, lambda: lat_relay(1))
-    for d in range(3, ctx_n):
-        when(ctx >= d, lambda d=d: lat_fetch(d))
-    lat_finish(0)
-    split_out()
     lat_ready(0)
     attend(0, 0)
+    split_out()
     for d in range(2, ctx_n):
         when(ctx >= d, lambda d=d: lat_relay(d))
     for q in range(1, chunks):
-        for copy in hid_direct(q):
-            copy.start()
-    attend_all(0, True)
-    for q in range(1, chunks):
         hid_relay(q)
+        hid_direct(q, REST[:2])
+    for d in late:
+        attend_late(0, d, True)
     project(0)
     for q in range(1, chunks):
         queries(q)
+        attend(q, 0)
+        for d in late[:1]:
+            attend_late(q, d, False)
         second_stage(q - 1)
-        attend(q, 0)
-        attend_all(q, False)
+        for d in late[1:]:
+            attend_late(q, d, False)
         project(q)
         collect(q - 1)
     second_stage(chunks - 1)
     collect(chunks - 1)
 
-    for q in range(chunks):
-        for copy in hid_direct(q) + [hid_passed(q, h) for h in range(2)]:
-            copy.wait_send()
-        for t in range(cuts[q]):
-            for j in range(3):
-                sum_copy(q, t, j).wait_send()
-            out_copy(q, t).wait()
+    sent = hid.at[pl.ds(0, 3 * rows)]
+    for sem in (hid_send.at[0], sum_send.at[0]):
+        remote(sent, sent, sem, hid_recv.at[0, 0], twin).wait_send()
+    local(res, out, out_sem.at[0]).wait()
     for d in range(ctx_n):
         def drain(d=d):
-            for copy in lat_direct(d) + [lat_passed(d, h) for h in range(2)] + [twin_own(d), twin_rest(d)]:
-                copy.wait_send()
+            sent = lat.at[pl.ds(0, (4 if d == 1 else 7) * slot)]
+            remote(sent, sent, lat_send.at[d], twin_recv.at[d], twin).wait_send()
+
+        def z_drain(d=d):
+            sent = lat.at[pl.ds(0, (4 if d == 1 else 1) * slot)]
+            remote(sent, sent, z_send.at[d - 1], z_recv.at[d - 1], head).wait_send()
 
         when(d <= ctx, drain)
         if d > 0:
-            when(ctx + d < ctx_n, lambda d=d: z_copy(d).wait_send())
+            when(ctx + d < ctx_n, z_drain)
 
 
 def square_call(ctx_n, hidden, w_query, w_down, gain, w_key_up, w_value_up, w_out):
@@ -767,15 +778,15 @@
             pltpu.VMEM((block, rank), f32),
             pltpu.VMEM((4 * rows, width), f32),
         ] + [pltpu.VMEM((rows, width), f32)] * 5 + [
-            dma((2 + steps + 4 + chunks,)),
-            dma((chunks, max(cuts))),
-            dma((4,)), dma((4,)),
-            dma((chunks, 3, 2)), dma((chunks, 3, 2)),
-            pltpu.SemaphoreType.REGULAR((ctx_n,)),
-            dma((ctx_n,)), dma((ctx_n,)),
-            dma((ctx_n, 3, 2)), dma((ctx_n, 3, 2)),
-            dma((ctx_n, 2)), dma((ctx_n, 2)),
-            dma((chunks, max(cuts), 3)), dma((chunks, max(cuts), 3)),
+            dma((6 + steps,)),
+            dma((1,)),
+            dma((3,)), dma((3,)),
+            dma((1,)), dma((chunks, 3)),
+            pltpu.SemaphoreType.REGULAR((max(ctx_n - 2, 1),)),
+            dma((max(ctx_n - 1, 1),)), dma((max(ctx_n - 1, 1),)),
+            dma((ctx_n,)), dma((ctx_n, 3)),
+            dma((ctx_n,)),
+            dma((1,)), dma((sum(cuts), 2)),
         ],
         compiler_params=pltpu.CompilerParams(
             collective_id=0, has_side_effects=True, vmem_limit_bytes=60 * 1024 * 1024

time: 48 us -> 41.2 us (0.86); the launches traced: 47.8 us -> 40.5 us
  Pallas kernels: 46.1 us -> 38.8 us
    pallas_call x1, Pallas kernels: 46.1 us -> 38.8 us  [square_call(): pl.pallas_call(functools.partial(square_kernel, ctx_n, chunks, cuts), out...]
where the time goes in v2:
time: 41.2 us; the launch traced here: 40.5 us
  Pallas kernels  38.8 us (94%)
  local copies, waits for them, and re-layouts  1.69 us (4%)
    pallas_call x1, Pallas kernels, square_call(): pl.pallas_call(functools.partial(square_kernel, ctx_n, chunks, cuts), out...  38.8 us
    unnamed x1, local copies, waits for them, and re-layouts  1.69 us

profile of v2, /device:TPU:24, one launch (start us, length us, event | category | flops | bytes accessed | tf_op | source)
XLA Modules:
  0.0 40.5 jit_solution(11967753088009127769)
XLA Ops:
  0.0 38.8 %shard_map.73 = f32[32,2304]{1,0:T(8,128)} custom-call(f32[32,2304]{1,0:T(8,128)} %hidden.1, f32[192,2304]{1,0:T(8,128)} %bitcast.4, f32[576,2304]{1,0:T(8,128)} %bitcast.3, f32[1,512]{1,0:T(1,128)} %bitcast.5, f32[512,128]{1,0:T(8,128)} %w_key.1, f32[512,128]{1,0:T(8,128)} %w_value.1, f32[128,2304]{1,0:T(8,128)} %w_out.1), custom_call_target="tpu_custom_call" | custom-call | tf_op jit(solution)/shard_map/pallas_call | solution.py:759
  38.8 1.7 %copy.9 = f32[32,2304]{1,0:T(8,128)} copy(f32[32,2304]{1,0:T(8,128)} %shard_map.73) | data formatting | bytes 589824

commit v3 on v2

--- a/solution.py
+++ b/solution.py
@@ -353,8 +353,8 @@
     ctx_n, chunks, cuts,
     hidden, w_query, w_down, gain, w_key, w_value, w_out, out,
     mine, hid, wd, gn, wq, wqh, wql, wk, wv, wo, woh, wol, lat, kh, kl, qh, ql, top, total, acc,
-    part, mid, fwd, near, last, res,
-    load_sem, out_sem, swap_send, swap_recv, hid_send, hid_recv, far_sem, z_send, z_recv,
+    part, mid, fwd, near, last,
+    load_sem, swap_send, swap_recv, hid_send, hid_recv, far_sem, z_send, z_recv,
     lat_send, lat_recv, twin_recv, sum_send, sum_recv,
 ):
     rows, width = hidden.shape
@@ -538,15 +538,10 @@
     lat_relay(0)
     if ctx_n > 1:
         when(ctx + 1 < ctx_n, z_begin)
-    for q in range(1, chunks):
-        hid_direct(q, FIRST)
     swaps[0].wait()
     split_query(1)
     for d in range(2, ctx_n):
         when(ctx >= d, lambda d=d: lat_fetch(d))
-    lat_finish(0)
-    if ctx_n > 1:
-        when(ctx + 1 < ctx_n, z_end)
     kept(1)
     local(mine, mine, load_sem.at[5 + steps]).wait()
 
@@ -593,18 +588,21 @@
         x, y = lax.rem(xbit + sx, 2), lax.rem(ybit + sy, 2)
         return ((2 * y + x) * CORES + parity) * rows + i
 
-    def attend(q, d):
+    def causal_of(q, count):
+        line = lax.rem(lax.broadcasted_iota(jnp.int32, (many, 1), 0), group)
+        column = lax.broadcasted_iota(jnp.int32, (1, count * block), 1)
+        there = lax.rem(lax.div(column, 4 * rows), CORES)
+        inner = lax.rem(column, 4 * rows)
+        asked = place(lax.div(line, r), core, q * r + lax.rem(line, r))
+        held = place(lax.div(inner, rows), core + there - 2 * core * there, lax.rem(inner, rows))
+        return asked >= jnp.where(column < block, held, -1)
+
+    def attend(q, d, count=1):
         mine_q = pl.ds(q * many, many)
-        those = pl.ds(d * block, block)
+        those = pl.ds(d * block, count * block)
         scores = stacked((qh[mine_q, :], ql[mine_q, :]), (kh[those, :], kl[those, :]), NT)
         if d == 0:
-            line = lax.rem(lax.broadcasted_iota(jnp.int32, (many, 1), 0), group)
-            column = lax.broadcasted_iota(jnp.int32, (1, block), 1)
-            there = lax.div(column, 4 * rows)
-            column = lax.rem(column, 4 * rows)
-            asked = place(lax.div(line, r), core, q * r + lax.rem(line, r))
-            held = place(lax.div(column, rows), core + there - 2 * core * there, lax.rem(column, rows))
-            causal = asked >= held
+            causal = causal_of(q, count)
             scores = jnp.where(causal, scores, FLOOR)
             peak = jnp.max(scores, axis=1, keepdims=True)
         else:
@@ -623,9 +621,13 @@
             acc[mine_q, :] = acc[mine_q, :] * fade + mixed
         top[mine_q, :] = peak
 
+    def attend_whole(q):
+        for count in range(1, ctx_n + 1):
+            when(ctx + 1 == count, lambda count=count: attend(q, 0, count))
+
     def span_of(q, t):
-        columns = width // cuts[q]
-        return pl.ds(t * columns, columns)
+        low, high = [width // 2 // LANE * i // cuts[q] * LANE for i in (t // 2, t // 2 + 1)]
+        return pl.ds(2 * low + t % 2 * (high - low), high - low)
 
     def axes_of(t):
         return (1, 2) if t % 2 == 0 else (2, 1)
@@ -643,7 +645,7 @@
             (part_of(first), near.at[here, span], first),
             (fwd.at[here, span], last.at[here, span], second),
         ][j]
-        return remote(src, dst, sum_send.at[0], sum_recv.at[sum(cuts[:q]) + t, min(j, 1)], side[target])
+        return remote(src, dst, sum_send.at[0], sum_recv.at[2 * sum(cuts[:q]) + t, min(j, 1)], side[target])
 
     def project(q):
         found = []
@@ -651,46 +653,29 @@
             span = pl.ds(q * many + p * group, group)
             found.append(stacked(halves(acc[span, :] / total[span, :]), halves(wv[p])))
         attended = halves(jnp.concatenate(found, axis=1))
-        for t in range(cuts[q]):
+        for t in range(2 * cuts[q]):
             span = span_of(q, t)
             part[pl.ds(q * group, group), span] = stacked(attended, (woh[:, span], wol[:, span]))
-            for j in range(2):
-                sum_copy(q, t, j).start()
+            sum_copy(q, t, 0).start()
+        for t in range(2 * cuts[q]):
+            sum_copy(q, t, 1).start()
 
     def second_stage(q):
         here = pl.ds(q * r, r)
-        for t in range(cuts[q]):
+        for t in range(2 * cuts[q]):
             span = span_of(q, t)
             sum_copy(q, t, 0).wait_recv()
             keep = axes_of(t)[1]
             fwd[here, span] = part[pl.ds(q * group + keep * r, r), span] + mid[here, span]
             sum_copy(q, t, 2).start()
 
-    def out_copy(q, t):
-        here, span = pl.ds(q * r, r), span_of(q, t)
-        return local(res.at[here, span], out.at[here, span], out_sem.at[0])
-
     def collect(q):
         here = pl.ds(q * r, r)
-        for t in range(cuts[q]):
+        for t in range(2 * cuts[q]):
             span = span_of(q, t)
             landed = near.at[pl.ds(0, 2 * r), span]
-            remote(landed, landed, sum_send.at[0], sum_recv.at[sum(cuts[:q]) + t, 1], twin).wait_recv()
-            res[here, span] = part[pl.ds(q * group, r), span] + near[here, span] + last[here, span]
-            out_copy(q, t).start()
-
-    def attend_late(q, d, ready):
-        def step():
-            if ready and d == 1:
-                z_wait(1)
-                lat_twin(1, 0, 4)
-            elif ready:
-                lat_finish(d)
-            if ready:
-                lat_ready(d)
-            attend(q, d)
-
-        when(d <= ctx, step)
+            remote(landed, landed, sum_send.at[0], sum_recv.at[2 * sum(cuts[:q]) + t, 1], twin).wait_recv()
+            out[here, span] = part[pl.ds(q * group, r), span] + near[here, span] + last[here, span]
 
     def split_out():
         kept(2)
@@ -698,27 +683,47 @@
             span = pl.ds(p * vdim, vdim)
             woh[span, :], wol[span, :] = halves(wo[p])
 
-    late = list(range(2, ctx_n)) + [1] * (ctx_n > 1)
+    def join(d):
+        lat_ready(d)
+        attend(0, d)
+
+    def z_join():
+        z_wait(1)
+        lat_twin(1, 0, 4)
+
+    def begin(d):
+        when(ctx >= d, lambda: lat_relay(d))
+
     queries(0)
-    lat_ready(0)
-    attend(0, 0)
+    lat_finish(0)
+    if ctx_n > 1:
+        when(ctx + 1 < ctx_n, z_end)
+    if ctx_n > 2:
+        begin(2)
+    for q in range(1, chunks):
+        hid_direct(q, FIRST)
+    join(0)
+    for d in range(3, ctx_n):
+        begin(d)
+    for q in range(1, chunks):
+        hid_direct(q, REST[:2])
     split_out()
-    for d in range(2, ctx_n):
-        when(ctx >= d, lambda d=d: lat_relay(d))
+    if ctx_n > 2:
+        when(ctx >= 2, lambda: lat_finish(2))
+        when(ctx >= 2, lambda: join(2))
+    if ctx_n > 1:
+        when(ctx >= 1, z_join)
     for q in range(1, chunks):
         hid_relay(q)
-        hid_direct(q, REST[:2])
-    for d in late:
-        attend_late(0, d, True)
+    for d in range(3, ctx_n):
+        when(ctx >= d, lambda d=d: lat_finish(d))
+    for d in [1] * (ctx_n > 1) + list(range(3, ctx_n)):
+        when(ctx >= d, lambda d=d: join(d))
     project(0)
     for q in range(1, chunks):
         queries(q)
-        attend(q, 0)
-        for d in late[:1]:
-            attend_late(q, d, False)
+        attend_whole(q)
         second_stage(q - 1)
-        for d in late[1:]:
-            attend_late(q, d, False)
         project(q)
         collect(q - 1)
     second_stage(chunks - 1)
@@ -727,7 +732,6 @@
     sent = hid.at[pl.ds(0, 3 * rows)]
     for sem in (hid_send.at[0], sum_send.at[0]):
         remote(sent, sent, sem, hid_recv.at[0, 0], twin).wait_send()
-    local(res, out, out_sem.at[0]).wait()
     for d in range(ctx_n):
         def drain(d=d):
             sent = lat.at[pl.ds(0, (4 if d == 1 else 7) * slot)]
@@ -748,7 +752,7 @@
     vdim = w_value_up.shape[1]
     f32, bf16, dma = jnp.float32, jnp.bfloat16, pltpu.SemaphoreType.DMA
     chunks = 2
-    cuts = (2, 6)
+    cuts = (1, 2)
     r = rows // chunks
     block = CORES * 4 * rows
     lanes = rank + LANE
@@ -758,9 +762,9 @@
     both = (CORES * vdim, width)
     return pl.pallas_call(
         functools.partial(square_kernel, ctx_n, chunks, cuts),
-        out_shape=jax.ShapeDtypeStruct((rows, width), f32),
+        out_shape=pltpu.VMEM((rows, width), f32),
         in_specs=[pl.BlockSpec(memory_space=pltpu.HBM)] * 7,
-        out_specs=pl.BlockSpec(memory_space=pltpu.HBM),
+        out_specs=pl.BlockSpec(memory_space=pltpu.VMEM),
         scratch_shapes=[
             pltpu.VMEM((rows, width), f32),
             pltpu.VMEM((4 * rows, width), f32),
@@ -777,16 +781,15 @@
             pltpu.VMEM((block, 1), f32),
             pltpu.VMEM((block, rank), f32),
             pltpu.VMEM((4 * rows, width), f32),
-        ] + [pltpu.VMEM((rows, width), f32)] * 5 + [
+        ] + [pltpu.VMEM((rows, width), f32)] * 4 + [
             dma((6 + steps,)),
-            dma((1,)),
             dma((3,)), dma((3,)),
             dma((1,)), dma((chunks, 3)),
             pltpu.SemaphoreType.REGULAR((max(ctx_n - 2, 1),)),
             dma((max(ctx_n - 1, 1),)), dma((max(ctx_n - 1, 1),)),
             dma((ctx_n,)), dma((ctx_n, 3)),
             dma((ctx_n,)),
-            dma((1,)), dma((sum(cuts), 2)),
+            dma((1,)), dma((2 * sum(cuts), 2)),
         ],
         compiler_params=pltpu.CompilerParams(
             collective_id=0, has_side_effects=True, vmem_limit_bytes=60 * 1024 * 1024

time: 41.2 us -> 36.5 us (0.89); the launches traced: 40.5 us -> 36.4 us
  Pallas kernels: 38.8 us -> 35.6 us
  local copies, waits for them, and re-layouts: 1.69 us -> 0.72 us
    pallas_call x1, Pallas kernels: 38.8 us -> 35.6 us  [square_call(): pl.pallas_call(functools.partial(square_kernel, ctx_n, chunks, cuts), out...]
    unnamed x1, local copies, waits for them, and re-layouts: 1.69 us -> 0.72 us
where the time goes in v3:
time: 36.5 us; the launch traced here: 36.4 us
  Pallas kernels  35.6 us (98%)
  local copies, waits for them, and re-layouts  0.72 us (2%)
    pallas_call x1, Pallas kernels, square_call(): pl.pallas_call(functools.partial(square_kernel, ctx_n, chunks, cuts), out...  35.6 us

profile of v3, /device:TPU:24, one launch (start us, length us, event | category | flops | bytes accessed | tf_op | source)
XLA Modules:
  0.0 36.4 jit_solution(14741711846892880234)
XLA Ops:
  0.0 35.6 %shard_map.73 = f32[32,2304]{1,0:T(8,128)S(1)} custom-call(f32[32,2304]{1,0:T(8,128)} %hidden.1, f32[192,2304]{1,0:T(8,128)} %bitcast.4, f32[576,2304]{1,0:T(8,128)} %bitcast.3, f32[1,512]{1,0:T(1,128)} %bitcast.5, f32[512,128]{1,0:T(8,128)} %w_key.1, f32[512,128]{1,0:T(8,128)} %w_value.1, f32[128,2304]{1,0:T(8,128)} %w_out.1), custom_call_target="tpu_custom_call" | custom-call | tf_op jit(solution)/shard_map/pallas_call | solution.py:763
  35.6 0.7 %copy.9 = f32[32,2304]{1,0:T(8,128)} copy(f32[32,2304]{1,0:T(8,128)S(1)} %shard_map.73) | data formatting | bytes 589824

commit v4 on v3

--- a/solution.py
+++ b/solution.py
@@ -352,7 +352,7 @@
 def square_kernel(
     ctx_n, chunks, cuts,
     hidden, w_query, w_down, gain, w_key, w_value, w_out, out,
-    mine, hid, wd, gn, wq, wqh, wql, wk, wv, wo, woh, wol, lat, kh, kl, qh, ql, top, total, acc,
+    mine, hid, wd, gn, wq, wqh, wql, wk, wv, wo, woh, wol, lat, kh, kl, qh, ql, total, acc,
     part, mid, fwd, near, last,
     load_sem, swap_send, swap_recv, hid_send, hid_recv, far_sem, z_send, z_recv,
     lat_send, lat_recv, twin_recv, sum_send, sum_recv,
@@ -434,17 +434,17 @@
         landed = lat_at(d, 0, 0, 0, 4 * slot if d == 1 else slot)
         remote(landed, landed, z_send.at[d - 1], z_recv.at[d - 1], head).wait_recv()
 
-    def lat_spread(d):
-        for a, h in DIRECT:
+    def lat_direct(d, order):
+        for a, h in order:
             remote(
                 lat_at(d, 0, 0, h), lat_at(d, 0, a, h), lat_send.at[d],
                 lat_recv.at[d, h if (a, h) in FIRST else 2], side[a],
             ).start()
-        lat_twin(d, 0, 1)
 
     def lat_fetch(d):
         z_wait(d)
-        lat_spread(d)
+        lat_direct(d, FIRST)
+        lat_twin(d, 0, 1)
 
     def lat_relay(d):
         for h in range(2):
@@ -456,7 +456,6 @@
         landed = lat_at(d, 0, 1, 0, 2 * slot)
         remote(landed, landed, lat_send.at[d], lat_recv.at[d, 2], twin).wait_recv()
         lat_twin(d, 1, 3)
-
     def z_begin():
         z_copy(1, 0, 0, slot).start()
         z_copy(1, 1, 0, piece).start()
@@ -522,7 +521,8 @@
             )
     for d in range(ctx_n - 1, 1, -1):
         when(ctx + d < ctx_n, lambda d=d: z_copy(d, 0, 0, slot).start())
-    lat_spread(0)
+    lat_direct(0, DIRECT)
+    lat_twin(0, 0, 1)
 
     def split_query(p):
         wqh[p], wql[p] = halves(wq[p])
@@ -542,6 +542,10 @@
     split_query(1)
     for d in range(2, ctx_n):
         when(ctx >= d, lambda d=d: lat_fetch(d))
+    for d in range(2, ctx_n):
+        when(ctx >= d, lambda d=d: lat_direct(d, REST[:2]))
+    for q in range(1, chunks):
+        when(jnp.logical_or(ctx < 2, core == 0), lambda q=q: hid_direct(q, FIRST))
     kept(1)
     local(mine, mine, load_sem.at[5 + steps]).wait()
 
@@ -563,25 +567,24 @@
             rest = jnp.concatenate([query[p][:, nope:] * scale, pad], axis=1)
             qh[span, rank:], ql[span, rank:] = halves(rest)
 
-    def keys(d):
-        for p in range(CORES):
-            for s in range(4):
-                at = d * block + (p * 4 + s) * rows
-                packed = jnp.concatenate(
-                    [lat_at(d, p, s, h)[pl.ds(tiles * hr, hr // 2), :] for h in range(2)], axis=0
-                )
-                for h in range(2):
-                    span = pl.ds(at + h * hr, hr)
-                    for j in range(tiles):
-                        lane = pl.ds(j * LANE, LANE)
-                        kh[span, lane], kl[span, lane] = halves(lat_at(d, p, s, h)[pl.ds(j * hr, hr), :])
-                    lane = pl.ds(rank, LANE)
-                    kh[span, lane], kl[span, lane] = halves(packed if h == 0 else pltpu.roll(packed, tail, 1))
+    def keys(d, p):
+        for s in range(4):
+            at = d * block + (p * 4 + s) * rows
+            packed = jnp.concatenate(
+                [lat_at(d, p, s, h)[pl.ds(tiles * hr, hr // 2), :] for h in range(2)], axis=0
+            )
+            for h in range(2):
+                span = pl.ds(at + h * hr, hr)
+                for j in range(tiles):
+                    lane = pl.ds(j * LANE, LANE)
+                    kh[span, lane], kl[span, lane] = halves(lat_at(d, p, s, h)[pl.ds(j * hr, hr), :])
+                lane = pl.ds(rank, LANE)
+                kh[span, lane], kl[span, lane] = halves(packed if h == 0 else pltpu.roll(packed, tail, 1))
 
     def lat_ready(d):
         landed = lat_at(d, 1, 0, 0, 4 * slot)
         remote(landed, landed, lat_send.at[d], twin_recv.at[d], twin).wait_recv()
-        keys(d)
+        keys(d, 1)
 
     def place(s, parity, i):
         sx, sy = lax.rem(s, 2), lax.div(s, 2)
@@ -597,33 +600,20 @@
         held = place(lax.div(inner, rows), core + there - 2 * core * there, lax.rem(inner, rows))
         return asked >= jnp.where(column < block, held, -1)
 
-    def attend(q, d, count=1):
+    def attend(q, count, between):
         mine_q = pl.ds(q * many, many)
-        those = pl.ds(d * block, count * block)
+        those = pl.ds(0, count * block)
         scores = stacked((qh[mine_q, :], ql[mine_q, :]), (kh[those, :], kl[those, :]), NT)
-        if d == 0:
-            causal = causal_of(q, count)
-            scores = jnp.where(causal, scores, FLOOR)
-            peak = jnp.max(scores, axis=1, keepdims=True)
-        else:
-            peak = jnp.maximum(top[mine_q, :], jnp.max(scores, axis=1, keepdims=True))
-        weights = jnp.exp(scores - peak)
-        if d == 0:
-            weights = jnp.where(causal, weights, 0.0)
-        mixed = stacked(halves(weights), (kh[those, :rank], kl[those, :rank]))
-        added = jnp.sum(weights, axis=1, keepdims=True)
-        if d == 0:
-            total[mine_q, :] = added
-            acc[mine_q, :] = mixed
-        else:
-            fade = jnp.exp(top[mine_q, :] - peak)
-            total[mine_q, :] = total[mine_q, :] * fade + added
-            acc[mine_q, :] = acc[mine_q, :] * fade + mixed
-        top[mine_q, :] = peak
-
-    def attend_whole(q):
+        causal = causal_of(q, count)
+        scores = jnp.where(causal, scores, FLOOR)
+        weights = jnp.where(causal, jnp.exp(scores - jnp.max(scores, axis=1, keepdims=True)), 0.0)
+        between()
+        total[mine_q, :] = jnp.sum(weights, axis=1, keepdims=True)
+        acc[mine_q, :] = stacked(halves(weights), (kh[those, :rank], kl[those, :rank]))
+
+    def attend_whole(q, between=lambda: None):
         for count in range(1, ctx_n + 1):
-            when(ctx + 1 == count, lambda count=count: attend(q, 0, count))
+            when(ctx + 1 == count, lambda count=count: attend(q, count, between))
 
     def span_of(q, t):
         low, high = [width // 2 // LANE * i // cuts[q] * LANE for i in (t // 2, t // 2 + 1)]
@@ -683,10 +673,6 @@
             span = pl.ds(p * vdim, vdim)
             woh[span, :], wol[span, :] = halves(wo[p])
 
-    def join(d):
-        lat_ready(d)
-        attend(0, d)
-
     def z_join():
         z_wait(1)
         lat_twin(1, 0, 4)
@@ -694,31 +680,37 @@
     def begin(d):
         when(ctx >= d, lambda: lat_relay(d))
 
+    def done(d):
+        lat_finish(d)
+        keys(d, 0)
+
+    def z_done():
+        z_join()
+        keys(1, 0)
+
     queries(0)
-    lat_finish(0)
+    done(0)
     if ctx_n > 1:
         when(ctx + 1 < ctx_n, z_end)
-    if ctx_n > 2:
-        begin(2)
-    for q in range(1, chunks):
-        hid_direct(q, FIRST)
-    join(0)
-    for d in range(3, ctx_n):
+    for d in range(2, ctx_n):
         begin(d)
     for q in range(1, chunks):
-        hid_direct(q, REST[:2])
+        when(jnp.logical_or(ctx < 2, core == 0), lambda q=q: hid_direct(q, REST[:2]))
     split_out()
     if ctx_n > 2:
-        when(ctx >= 2, lambda: lat_finish(2))
-        when(ctx >= 2, lambda: join(2))
+        when(ctx >= 2, lambda: done(2))
     if ctx_n > 1:
-        when(ctx >= 1, z_join)
+        when(ctx >= 1, z_done)
+    for d in range(3, ctx_n):
+        when(ctx >= d, lambda d=d: done(d))
+    for q in range(1, chunks):
+        when(jnp.logical_and(ctx >= 2, core == 1), lambda q=q: hid_direct(q, FIRST + REST[:2]))
     for q in range(1, chunks):
         hid_relay(q)
-    for d in range(3, ctx_n):
-        when(ctx >= d, lambda d=d: lat_finish(d))
-    for d in [1] * (ctx_n > 1) + list(range(3, ctx_n)):
-        when(ctx >= d, lambda d=d: join(d))
+    lat_ready(0)
+    for d in range(1, ctx_n):
+        when(ctx >= d, lambda d=d: lat_ready(d))
+    attend_whole(0)
     project(0)
     for q in range(1, chunks):
         queries(q)
@@ -777,7 +769,6 @@
             pltpu.VMEM((ctx_n * CORES * 4 * slot, LANE), f32),
             pltpu.VMEM((ctx_n * block, lanes), bf16), pltpu.VMEM((ctx_n * block, lanes), bf16),
             pltpu.VMEM((block, lanes), bf16), pltpu.VMEM((block, lanes), bf16),
-            pltpu.VMEM((block, 1), f32),
             pltpu.VMEM((block, 1), f32),
             pltpu.VMEM((block, rank), f32),
             pltpu.VMEM((4 * rows, width), f32),

time: 36.5 us -> 34.9 us (0.956)
  Pallas kernels: 35.6 us -> 33.7 us
    pallas_call x1, Pallas kernels: 35.6 us -> 33.7 us  [square_call(): pl.pallas_call(functools.partial(square_kernel, ctx_n, chunks, cuts), out...]
where the time goes in v4:
time: 34.9 us; the launch traced here: 34.5 us
  Pallas kernels  33.7 us (97%)
  local copies, waits for them, and re-layouts  0.72 us (2%)
    pallas_call x1, Pallas kernels, square_call(): pl.pallas_call(functools.partial(square_kernel, ctx_n, chunks, cuts), out...  33.7 us
    unnamed x1, local copies, waits for them, and re-layouts  0.72 us

profile of v4, /device:TPU:24, one launch (start us, length us, event | category | flops | bytes accessed | tf_op | source)
XLA Modules:
  0.0 34.5 jit_solution(12800425065005843334)
XLA Ops:
  0.0 33.7 %shard_map.73 = f32[32,2304]{1,0:T(8,128)S(1)} custom-call(f32[32,2304]{1,0:T(8,128)} %hidden.1, f32[192,2304]{1,0:T(8,128)} %bitcast.4, f32[576,2304]{1,0:T(8,128)} %bitcast.3, f32[1,512]{1,0:T(1,128)} %bitcast.5, f32[512,128]{1,0:T(8,128)} %w_key.1, f32[512,128]{1,0:T(8,128)} %w_value.1, f32[128,2304]{1,0:T(8,128)} %w_out.1), custom_call_target="tpu_custom_call" | custom-call | tf_op jit(solution)/shard_map/pallas_call | solution.py:755
  33.8 0.7 %copy.9 = f32[32,2304]{1,0:T(8,128)} copy(f32[32,2304]{1,0:T(8,128)S(1)} %shard_map.73) | data formatting | bytes 589824

commit v5 on v4

--- a/solution.py
+++ b/solution.py
@@ -484,7 +484,7 @@
     when(ctx + 1 < ctx_n, lambda: signal(barrier, ctx + 1, head))
     pl.semaphore_wait(barrier, 3 + jnp.minimum(ctx, 1) + jnp.minimum(ctx_n - 1 - ctx, 1))
 
-    hid_direct(0, FIRST + REST[:2])
+    hid_direct(0, FIRST)
     swaps = [
         remote(src, dst.at[1], swap_send.at[lot], swap_recv.at[lot], twin) for (src, dst), lot in zip(pairs, lots)
     ]
@@ -522,6 +522,7 @@
     for d in range(ctx_n - 1, 1, -1):
         when(ctx + d < ctx_n, lambda d=d: z_copy(d, 0, 0, slot).start())
     lat_direct(0, DIRECT)
+    hid_direct(0, REST[:2])
     lat_twin(0, 0, 1)
 
     def split_query(p):
@@ -637,7 +638,7 @@
         ][j]
         return remote(src, dst, sum_send.at[0], sum_recv.at[2 * sum(cuts[:q]) + t, min(j, 1)], side[target])
 
-    def project(q):
+    def project(q, between=lambda: None):
         found = []
         for p in range(CORES):
             span = pl.ds(q * many + p * group, group)
@@ -647,12 +648,13 @@
             span = span_of(q, t)
             part[pl.ds(q * group, group), span] = stacked(attended, (woh[:, span], wol[:, span]))
             sum_copy(q, t, 0).start()
+        between()
         for t in range(2 * cuts[q]):
             sum_copy(q, t, 1).start()
 
-    def second_stage(q):
+    def second_stage(q, low, high):
         here = pl.ds(q * r, r)
-        for t in range(2 * cuts[q]):
+        for t in range(low, high):
             span = span_of(q, t)
             sum_copy(q, t, 0).wait_recv()
             keep = axes_of(t)[1]
@@ -715,10 +717,10 @@
     for q in range(1, chunks):
         queries(q)
         attend_whole(q)
-        second_stage(q - 1)
-        project(q)
+        second_stage(q - 1, 0, 2)
+        project(q, lambda: second_stage(q - 1, 2, 2 * cuts[q - 1]))
+        second_stage(q, 0, 2 * cuts[q])
         collect(q - 1)
-    second_stage(chunks - 1)
     collect(chunks - 1)
 
     sent = hid.at[pl.ds(0, 3 * rows)]
@@ -744,7 +746,7 @@
     vdim = w_value_up.shape[1]
     f32, bf16, dma = jnp.float32, jnp.bfloat16, pltpu.SemaphoreType.DMA
     chunks = 2
-    cuts = (1, 2)
+    cuts = (2, 2)
     r = rows // chunks
     block = CORES * 4 * rows
     lanes = rank + LANE

time: 34.9 us -> 34.6 us (level)
  Pallas kernels: 33.7 us -> 33.3 us
    pallas_call x1, Pallas kernels: 33.7 us -> 33.3 us  [square_call(): pl.pallas_call(functools.partial(square_kernel, ctx_n, chunks, cuts), out...]
where the time goes in v5:
time: 34.6 us; the launch traced here: 34 us
  Pallas kernels  33.3 us (96%)
  local copies, waits for them, and re-layouts  0.72 us (2%)
    pallas_call x1, Pallas kernels, square_call(): pl.pallas_call(functools.partial(square_kernel, ctx_n, chunks, cuts), out...  33.3 us
    unnamed x1, local copies, waits for them, and re-layouts  0.72 us

profile of v5, /device:TPU:24, one launch (start us, length us, event | category | flops | bytes accessed | tf_op | source)
XLA Modules:
  0.0 34.0 jit_solution(16895013521043244539)
XLA Ops:
  0.0 33.3 %shard_map.73 = f32[32,2304]{1,0:T(8,128)S(1)} custom-call(f32[32,2304]{1,0:T(8,128)} %hidden.1, f32[192,2304]{1,0:T(8,128)} %bitcast.4, f32[576,2304]{1,0:T(8,128)} %bitcast.3, f32[1,512]{1,0:T(1,128)} %bitcast.5, f32[512,128]{1,0:T(8,128)} %w_key.1, f32[512,128]{1,0:T(8,128)} %w_value.1, f32[128,2304]{1,0:T(8,128)} %w_out.1), custom_call_target="tpu_custom_call" | custom-call | tf_op jit(solution)/shard_map/pallas_call | solution.py:757
  33.3 0.7 %copy.9 = f32[32,2304]{1,0:T(8,128)} copy(f32[32,2304]{1,0:T(8,128)S(1)} %shard_map.73) | data formatting | bytes 589824

commit v6 on v5

--- a/solution.py
+++ b/solution.py
@@ -424,7 +424,7 @@
 
     def lat_twin(d, s, count):
         size = count * slot
-        remote(lat_at(d, 0, s, 0, size), lat_at(d, 1, s, 0, size), lat_send.at[d], twin_recv.at[d], twin).start()
+        remote(lat_at(d, 0, s, 0, size), lat_at(d, 1, s, 0, size), lat_send.at[d], twin_recv.at[0], twin).start()
 
     def z_copy(d, s, h, size):
         c = jnp.minimum(ctx + d, ctx_n - 1)
@@ -438,7 +438,7 @@
         for a, h in order:
             remote(
                 lat_at(d, 0, 0, h), lat_at(d, 0, a, h), lat_send.at[d],
-                lat_recv.at[d, h if (a, h) in FIRST else 2], side[a],
+                lat_recv.at[max(d - 1, 0), h if (a, h) in FIRST else 2], side[a],
             ).start()
 
     def lat_fetch(d):
@@ -449,12 +449,12 @@
     def lat_relay(d):
         for h in range(2):
             landed = lat_at(d, 0, 1 + h, h)
-            remote(landed, landed, lat_send.at[d], lat_recv.at[d, h], twin).wait_recv()
-            remote(landed, lat_at(d, 0, 3, h), lat_send.at[d], lat_recv.at[d, 2], side[2 - h]).start()
+            remote(landed, landed, lat_send.at[d], lat_recv.at[max(d - 1, 0), h], twin).wait_recv()
+            remote(landed, lat_at(d, 0, 3, h), lat_send.at[d], lat_recv.at[max(d - 1, 0), 2], side[2 - h]).start()
 
     def lat_finish(d):
         landed = lat_at(d, 0, 1, 0, 2 * slot)
-        remote(landed, landed, lat_send.at[d], lat_recv.at[d, 2], twin).wait_recv()
+        remote(landed, landed, lat_send.at[d], lat_recv.at[max(d - 1, 0), 2], twin).wait_recv()
         lat_twin(d, 1, 3)
     def z_begin():
         z_copy(1, 0, 0, slot).start()
@@ -519,7 +519,7 @@
                 jnp.logical_and(ctx >= 1, ctx + d < ctx_n),
                 lambda d=d: signal(far_sem.at[d - 1], ctx - 1, head),
             )
-    for d in range(ctx_n - 1, 1, -1):
+    for d in range(2, ctx_n):
         when(ctx + d < ctx_n, lambda d=d: z_copy(d, 0, 0, slot).start())
     lat_direct(0, DIRECT)
     hid_direct(0, REST[:2])
@@ -582,10 +582,11 @@
                 lane = pl.ds(rank, LANE)
                 kh[span, lane], kl[span, lane] = halves(packed if h == 0 else pltpu.roll(packed, tail, 1))
 
-    def lat_ready(d):
-        landed = lat_at(d, 1, 0, 0, 4 * slot)
-        remote(landed, landed, lat_send.at[d], twin_recv.at[d], twin).wait_recv()
-        keys(d, 1)
+    def lat_ready(count):
+        landed = lat.at[pl.ds(0, 4 * count * slot)]
+        remote(landed, landed, lat_send.at[0], twin_recv.at[0], twin).wait_recv()
+        for d in range(count):
+            keys(d, 1)
 
     def place(s, parity, i):
         sx, sy = lax.rem(s, 2), lax.div(s, 2)
@@ -636,7 +637,7 @@
             (part_of(first), near.at[here, span], first),
             (fwd.at[here, span], last.at[here, span], second),
         ][j]
-        return remote(src, dst, sum_send.at[0], sum_recv.at[2 * sum(cuts[:q]) + t, min(j, 1)], side[target])
+        return remote(src, dst, sum_send.at[0], sum_recv.at[2 * sum(cuts[:q]) + t if j == 0 else 2 * sum(cuts) + q], side[target])
 
     def project(q, between=lambda: None):
         found = []
@@ -663,11 +664,9 @@
 
     def collect(q):
         here = pl.ds(q * r, r)
-        for t in range(2 * cuts[q]):
-            span = span_of(q, t)
-            landed = near.at[pl.ds(0, 2 * r), span]
-            remote(landed, landed, sum_send.at[0], sum_recv.at[2 * sum(cuts[:q]) + t, 1], twin).wait_recv()
-            out[here, span] = part[pl.ds(q * group, r), span] + near[here, span] + last[here, span]
+        landed = near.at[pl.ds(0, 2 * r)]
+        remote(landed, landed, sum_send.at[0], sum_recv.at[2 * sum(cuts) + q], twin).wait_recv()
+        out[here, :] = part[pl.ds(q * group, r), :] + near[here, :] + last[here, :]
 
     def split_out():
         kept(2)
@@ -690,10 +689,14 @@
         z_join()
         keys(1, 0)
 
+    def sent_on():
+        done(0)
+        if ctx_n > 1:
+            when(ctx + 1 < ctx_n, z_end)
+
+    when(ctx < 1, sent_on)
     queries(0)
-    done(0)
-    if ctx_n > 1:
-        when(ctx + 1 < ctx_n, z_end)
+    when(ctx >= 1, sent_on)
     for d in range(2, ctx_n):
         begin(d)
     for q in range(1, chunks):
@@ -709,16 +712,15 @@
         when(jnp.logical_and(ctx >= 2, core == 1), lambda q=q: hid_direct(q, FIRST + REST[:2]))
     for q in range(1, chunks):
         hid_relay(q)
-    lat_ready(0)
-    for d in range(1, ctx_n):
-        when(ctx >= d, lambda d=d: lat_ready(d))
+    for count in range(1, ctx_n + 1):
+        when(ctx + 1 == count, lambda count=count: lat_ready(count))
     attend_whole(0)
     project(0)
     for q in range(1, chunks):
         queries(q)
-        attend_whole(q)
-        second_stage(q - 1, 0, 2)
-        project(q, lambda: second_stage(q - 1, 2, 2 * cuts[q - 1]))
+        attend_whole(q, lambda: second_stage(q - 1, 0, 3))
+        second_stage(q - 1, 3, 2 * cuts[q - 1])
+        project(q)
         second_stage(q, 0, 2 * cuts[q])
         collect(q - 1)
     collect(chunks - 1)
@@ -729,7 +731,7 @@
     for d in range(ctx_n):
         def drain(d=d):
             sent = lat.at[pl.ds(0, (4 if d == 1 else 7) * slot)]
-            remote(sent, sent, lat_send.at[d], twin_recv.at[d], twin).wait_send()
+            remote(sent, sent, lat_send.at[d], twin_recv.at[0], twin).wait_send()
 
         def z_drain(d=d):
             sent = lat.at[pl.ds(0, (4 if d == 1 else 1) * slot)]
@@ -780,9 +782,9 @@
             dma((1,)), dma((chunks, 3)),
             pltpu.SemaphoreType.REGULAR((max(ctx_n - 2, 1),)),
             dma((max(ctx_n - 1, 1),)), dma((max(ctx_n - 1, 1),)),
-            dma((ctx_n,)), dma((ctx_n, 3)),
-            dma((ctx_n,)),
-            dma((1,)), dma((2 * sum(cuts), 2)),
+            dma((ctx_n,)), dma((max(ctx_n - 1, 1), 3)),
+            dma((1,)),
+            dma((1,)), dma((2 * sum(cuts) + chunks,)),
         ],
         compiler_params=pltpu.CompilerParams(
             collective_id=0, has_side_effects=True, vmem_limit_bytes=60 * 1024 * 1024

time: 34.6 us -> 34.1 us (0.986)
  Pallas kernels: 33.3 us -> 32.9 us
where the time goes in v6:
time: 34.1 us; the launch traced here: 33.7 us
  Pallas kernels  32.9 us (96%)
  local copies, waits for them, and re-layouts  0.72 us (2%)
    pallas_call x1, Pallas kernels, square_call(): pl.pallas_call(functools.partial(square_kernel, ctx_n, chunks, cuts), out...  32.9 us
    unnamed x1, local copies, waits for them, and re-layouts  0.72 us

profile of v6, /device:TPU:24, one launch (start us, length us, event | category | flops | bytes accessed | tf_op | source)
XLA Modules:
  0.0 33.7 jit_solution(13668979335395610898)
XLA Ops:
  0.0 32.9 %shard_map.73 = f32[32,2304]{1,0:T(8,128)S(1)} custom-call(f32[32,2304]{1,0:T(8,128)} %hidden.1, f32[192,2304]{1,0:T(8,128)} %bitcast.4, f32[576,2304]{1,0:T(8,128)} %bitcast.3, f32[1,512]{1,0:T(1,128)} %bitcast.5, f32[512,128]{1,0:T(8,128)} %w_key.1, f32[512,128]{1,0:T(8,128)} %w_value.1, f32[128,2304]{1,0:T(8,128)} %w_out.1), custom_call_target="tpu_custom_call" | custom-call | tf_op jit(solution)/shard_map/pallas_call | solution.py:759
  33.0 0.7 %copy.9 = f32[32,2304]{1,0:T(8,128)} copy(f32[32,2304]{1,0:T(8,128)S(1)} %shard_map.73) | data formatting | bytes 589824

commit v7 on v6

--- a/solution.py
+++ b/solution.py
@@ -748,7 +748,7 @@
     vdim = w_value_up.shape[1]
     f32, bf16, dma = jnp.float32, jnp.bfloat16, pltpu.SemaphoreType.DMA
     chunks = 2
-    cuts = (2, 2)
+    cuts = (2, 3)
     r = rows // chunks
     block = CORES * 4 * rows
     lanes = rank + LANE

time: 34.1 us -> 33.9 us (level)
  no operation moved by 1% of the time
where the time goes in v7:
time: 33.9 us; the launch traced here: 33.4 us
  Pallas kernels  32.6 us (96%)
  local copies, waits for them, and re-layouts  0.72 us (2%)
    pallas_call x1, Pallas kernels, square_call(): pl.pallas_call(functools.partial(square_kernel, ctx_n, chunks, cuts), out...  32.6 us
    unnamed x1, local copies, waits for them, and re-layouts  0.72 us

profile of v7, /device:TPU:24, one launch (start us, length us, event | category | flops | bytes accessed | tf_op | source)
XLA Modules:
  0.0 33.4 jit_solution(8371206313020318457)
XLA Ops:
  0.0 32.6 %shard_map.73 = f32[32,2304]{1,0:T(8,128)S(1)} custom-call(f32[32,2304]{1,0:T(8,128)} %hidden.1, f32[192,2304]{1,0:T(8,128)} %bitcast.4, f32[576,2304]{1,0:T(8,128)} %bitcast.3, f32[1,512]{1,0:T(1,128)} %bitcast.5, f32[512,128]{1,0:T(8,128)} %w_key.1, f32[512,128]{1,0:T(8,128)} %w_value.1, f32[128,2304]{1,0:T(8,128)} %w_out.1), custom_call_target="tpu_custom_call" | custom-call | tf_op jit(solution)/shard_map/pallas_call | solution.py:759
  32.6 0.7 %copy.9 = f32[32,2304]{1,0:T(8,128)} copy(f32[32,2304]{1,0:T(8,128)S(1)} %shard_map.73) | data formatting | bytes 589824

commit v8 on v7

--- a/solution.py
+++ b/solution.py
@@ -424,20 +424,20 @@
 
     def lat_twin(d, s, count):
         size = count * slot
-        remote(lat_at(d, 0, s, 0, size), lat_at(d, 1, s, 0, size), lat_send.at[d], twin_recv.at[0], twin).start()
+        remote(lat_at(d, 0, s, 0, size), lat_at(d, 1, s, 0, size), lat_send.at[0], twin_recv.at[0], twin).start()
 
     def z_copy(d, s, h, size):
         c = jnp.minimum(ctx + d, ctx_n - 1)
-        return remote(lat_at(0, 0, s, h, size), lat_at(d, 0, s, h, size), z_send.at[d - 1], z_recv.at[d - 1], head, c)
+        return remote(lat_at(0, 0, s, h, size), lat_at(d, 0, s, h, size), z_send.at[0], z_recv.at[d - 1], head, c)
 
     def z_wait(d):
         landed = lat_at(d, 0, 0, 0, 4 * slot if d == 1 else slot)
-        remote(landed, landed, z_send.at[d - 1], z_recv.at[d - 1], head).wait_recv()
+        remote(landed, landed, z_send.at[0], z_recv.at[d - 1], head).wait_recv()
 
     def lat_direct(d, order):
         for a, h in order:
             remote(
-                lat_at(d, 0, 0, h), lat_at(d, 0, a, h), lat_send.at[d],
+                lat_at(d, 0, 0, h), lat_at(d, 0, a, h), lat_send.at[0],
                 lat_recv.at[max(d - 1, 0), h if (a, h) in FIRST else 2], side[a],
             ).start()
 
@@ -449,12 +449,12 @@
     def lat_relay(d):
         for h in range(2):
             landed = lat_at(d, 0, 1 + h, h)
-            remote(landed, landed, lat_send.at[d], lat_recv.at[max(d - 1, 0), h], twin).wait_recv()
-            remote(landed, lat_at(d, 0, 3, h), lat_send.at[d], lat_recv.at[max(d - 1, 0), 2], side[2 - h]).start()
+            remote(landed, landed, lat_send.at[0], lat_recv.at[max(d - 1, 0), h], twin).wait_recv()
+            remote(landed, lat_at(d, 0, 3, h), lat_send.at[0], lat_recv.at[max(d - 1, 0), 2], side[2 - h]).start()
 
     def lat_finish(d):
         landed = lat_at(d, 0, 1, 0, 2 * slot)
-        remote(landed, landed, lat_send.at[d], lat_recv.at[max(d - 1, 0), 2], twin).wait_recv()
+        remote(landed, landed, lat_send.at[0], lat_recv.at[max(d - 1, 0), 2], twin).wait_recv()
         lat_twin(d, 1, 3)
     def z_begin():
         z_copy(1, 0, 0, slot).start()
@@ -728,18 +728,16 @@
     sent = hid.at[pl.ds(0, 3 * rows)]
     for sem in (hid_send.at[0], sum_send.at[0]):
         remote(sent, sent, sem, hid_recv.at[0, 0], twin).wait_send()
-    for d in range(ctx_n):
-        def drain(d=d):
-            sent = lat.at[pl.ds(0, (4 if d == 1 else 7) * slot)]
-            remote(sent, sent, lat_send.at[d], twin_recv.at[0], twin).wait_send()
-
-        def z_drain(d=d):
-            sent = lat.at[pl.ds(0, (4 if d == 1 else 1) * slot)]
-            remote(sent, sent, z_send.at[d - 1], z_recv.at[d - 1], head).wait_send()
-
-        when(d <= ctx, drain)
-        if d > 0:
-            when(ctx + d < ctx_n, z_drain)
+    for here in range(ctx_n):
+        def drain(here=here):
+            slots = 7 * (here + 1) - 3 * (here > 0)
+            sent = lat.at[pl.ds(0, slots * slot)]
+            remote(sent, sent, lat_send.at[0], twin_recv.at[0], twin).wait_send()
+            if here + 1 < ctx_n:
+                sent = lat.at[pl.ds(0, (ctx_n - here + 2) * slot)]
+                remote(sent, sent, z_send.at[0], z_recv.at[0], head).wait_send()
+
+        when(ctx == here, drain)
 
 
 def square_call(ctx_n, hidden, w_query, w_down, gain, w_key_up, w_value_up, w_out):
@@ -781,8 +779,8 @@
             dma((3,)), dma((3,)),
             dma((1,)), dma((chunks, 3)),
             pltpu.SemaphoreType.REGULAR((max(ctx_n - 2, 1),)),
-            dma((max(ctx_n - 1, 1),)), dma((max(ctx_n - 1, 1),)),
-            dma((ctx_n,)), dma((max(ctx_n - 1, 1), 3)),
+            dma((1,)), dma((max(ctx_n - 1, 1),)),
+            dma((1,)), dma((max(ctx_n - 1, 1), 3)),
             dma((1,)),
             dma((1,)), dma((2 * sum(cuts) + chunks,)),
         ],

time: 33.9 us -> 33.9 us (level)
  no operation moved by 1% of the time
where the time goes in v8:
time: 33.9 us; the launch traced here: 33.3 us
  Pallas kernels  32.6 us (96%)
  local copies, waits for them, and re-layouts  0.72 us (2%)
    pallas_call x1, Pallas kernels, square_call(): pl.pallas_call(functools.partial(square_kernel, ctx_n, chunks, cuts), out...  32.6 us
    unnamed x1, local copies, waits for them, and re-layouts  0.72 us

profile of v8, /device:TPU:24, one launch (start us, length us, event | category | flops | bytes accessed | tf_op | source)
XLA Modules:
  0.0 33.3 jit_solution(16906869987233765774)
XLA Ops:
  0.0 32.6 %shard_map.73 = f32[32,2304]{1,0:T(8,128)S(1)} custom-call(f32[32,2304]{1,0:T(8,128)} %hidden.1, f32[192,2304]{1,0:T(8,128)} %bitcast.4, f32[576,2304]{1,0:T(8,128)} %bitcast.3, f32[1,512]{1,0:T(1,128)} %bitcast.5, f32[512,128]{1,0:T(8,128)} %w_key.1, f32[512,128]{1,0:T(8,128)} %w_value.1, f32[128,2304]{1,0:T(8,128)} %w_out.1), custom_call_target="tpu_custom_call" | custom-call | tf_op jit(solution)/shard_map/pallas_call | solution.py:757
  32.6 0.7 %copy.9 = f32[32,2304]{1,0:T(8,128)} copy(f32[32,2304]{1,0:T(8,128)S(1)} %shard_map.73) | data formatting | bytes 589824

commit v9 on v8

--- a/solution.py
+++ b/solution.py
@@ -406,18 +406,18 @@
         for a, h in order:
             remote(
                 hidden.at[pl.ds(q * r, r), pl.ds(h * half, half)], spot(q, a, h),
-                hid_send.at[0], hid_recv.at[q, h if (a, h) in FIRST else 2], side[a],
+                hid_send.at[0], hid_recv.at[q, 0 if (a, h) in FIRST else 1], side[a],
             ).start()
 
     def hid_relay(q):
+        landed = hid.at[pl.ds((q * 4 + 1) * r, r)]
+        remote(landed, landed, hid_send.at[0], hid_recv.at[q, 0], twin).wait_recv()
         for h in range(2):
-            landed = spot(q, 1 + h, h)
-            remote(landed, landed, hid_send.at[0], hid_recv.at[q, h], twin).wait_recv()
-            remote(landed, spot(q, 3, h), hid_send.at[0], hid_recv.at[q, 2], side[2 - h]).start()
+            remote(spot(q, 1 + h, h), spot(q, 3, h), hid_send.at[0], hid_recv.at[q, 1], side[2 - h]).start()
 
     def hid_finish(q):
         landed = hid.at[pl.ds((q * 4 + 1) * r, 2 * r)]
-        remote(landed, landed, hid_send.at[0], hid_recv.at[q, 2], twin).wait_recv()
+        remote(landed, landed, hid_send.at[0], hid_recv.at[q, 1], twin).wait_recv()
 
     def lat_at(d, p, s, h=0, size=piece):
         return lat.at[pl.ds(((d * CORES + p) * 4 + s) * slot + h * piece, size)]
@@ -777,7 +777,7 @@
         ] + [pltpu.VMEM((rows, width), f32)] * 4 + [
             dma((6 + steps,)),
             dma((3,)), dma((3,)),
-            dma((1,)), dma((chunks, 3)),
+            dma((1,)), dma((chunks, 2)),
             pltpu.SemaphoreType.REGULAR((max(ctx_n - 2, 1),)),
             dma((1,)), dma((max(ctx_n - 1, 1),)),
             dma((1,)), dma((max(ctx_n - 1, 1), 3)),

time: 33.9 us -> 33.8 us (level)
  no operation moved by 1% of the time
where the time goes in v9:
time: 33.8 us; the launch traced here: 33.3 us
  Pallas kernels  32.6 us (96%)
  local copies, waits for them, and re-layouts  0.72 us (2%)
    pallas_call x1, Pallas kernels, square_call(): pl.pallas_call(functools.partial(square_kernel, ctx_n, chunks, cuts), out...  32.6 us
    unnamed x1, local copies, waits for them, and re-layouts  0.72 us

profile of v9, /device:TPU:24, one launch (start us, length us, event | category | flops | bytes accessed | tf_op | source)
XLA Modules:
  0.0 33.3 jit_solution(7950266240482485050)
XLA Ops:
  0.0 32.6 %shard_map.73 = f32[32,2304]{1,0:T(8,128)S(1)} custom-call(f32[32,2304]{1,0:T(8,128)} %hidden.1, f32[192,2304]{1,0:T(8,128)} %bitcast.4, f32[576,2304]{1,0:T(8,128)} %bitcast.3, f32[1,512]{1,0:T(1,128)} %bitcast.5, f32[512,128]{1,0:T(8,128)} %w_key.1, f32[512,128]{1,0:T(8,128)} %w_value.1, f32[128,2304]{1,0:T(8,128)} %w_out.1), custom_call_target="tpu_custom_call" | custom-call | tf_op jit(solution)/shard_map/pallas_call | solution.py:757
  32.6 0.7 %copy.9 = f32[32,2304]{1,0:T(8,128)} copy(f32[32,2304]{1,0:T(8,128)S(1)} %shard_map.73) | data formatting | bytes 589824
